TPU v7x, 512 devices: a whole 4x8x8 slice. The times are simulated.
512 devices in a mesh: dp: 8 (over z), expert: 64 (over x, y, core).
Axes of the slice: x: 4, y: 8, z: 8, core: 2. Of those that a mesh axis runs over, the one named last changes fastest.
Arguments:
- tokens: bfloat16 [65536, 1024], P(('dp', 'expert')), may hold values from -6 to 6
- d_output: bfloat16 [65536, 1024], P(('dp', 'expert')), may hold values from -6 to 6
- combine: float32 [65536, 8], P(('dp', 'expert')), may hold values from 0.05 to 1
- routes: int32 [65536, 8], P(('dp', 'expert')), may hold values from 0 to 63, all different within a row; in each aligned block of 128 rows (0 to 127, 128 to 255, ...) at most 18 rows name the same one
- gate_weight: bfloat16 [64, 1024, 384], P('expert', 'dp'), may hold values from -0.1875 to 0.1875
- up_weight: bfloat16 [64, 1024, 384], P('expert', 'dp'), may hold values from -0.1875 to 0.1875
- down_weight: bfloat16 [64, 384, 1024], P('expert', None, 'dp'), may hold values from -0.3125 to 0.3125
Outputs:
- d_tokens: bfloat16 [65536, 1024], P(('dp', 'expert'))
- d_gate_weight: float32 [64, 1024, 384], P('expert', 'dp')
- d_up_weight: float32 [64, 1024, 384], P('expert', 'dp')
- d_down_weight: float32 [64, 384, 1024], P('expert', None, 'dp')
Inputs may be any that keep to these rules, and one draw needn't show every extreme that they name: `routes`: among the 128 tokens of one device, each expert id is named by at most 18 rows; some expert is named by exactly 18 rows on some device. The ids of one token differ.
All inputs are finite; a program needn't handle non-finite values.
Results may differ from a plain program's by a relative error of at most 0.015.
Values may be sent and summed in bfloat16 or wider, within the bound.
A program may use at most 64 MiB of HBM per device.

v0:
```python
import jax
import jax.numpy as jnp
from jax import lax
from jax.sharding import PartitionSpec as P


def route_slots(routes, experts):
    matches = (routes[:, :, None] == jnp.arange(experts, dtype=jnp.int32)[None, None, :]).astype(
        jnp.int32
    )
    per_token = jnp.sum(matches, axis=1)
    earlier = jnp.cumsum(per_token, axis=0) - per_token
    return jnp.sum(matches * earlier[:, None, :], axis=2)


def row_work(row_inputs, row_grads, gate_up, down_matrix):
    hidden_units = down_matrix.shape[0]
    preact = jnp.dot(row_inputs, gate_up, preferred_element_type=jnp.float32)
    gate_pre = preact[:, :hidden_units]
    up_pre = preact[:, hidden_units:]
    gate_sigmoid = jax.nn.sigmoid(gate_pre)
    hidden = (gate_pre * gate_sigmoid * up_pre).astype(jnp.bfloat16)
    d_hidden = jnp.dot(row_grads, down_matrix.T, preferred_element_type=jnp.float32)
    d_gate_pre = d_hidden * up_pre * gate_sigmoid * (1.0 + gate_pre * (1.0 - gate_sigmoid))
    d_up_pre = d_hidden * gate_pre * gate_sigmoid
    d_preact = jnp.concatenate([d_gate_pre, d_up_pre], axis=1).astype(jnp.bfloat16)
    d_rows = jnp.dot(d_preact, gate_up.T, preferred_element_type=jnp.float32).astype(jnp.bfloat16)
    return (d_rows, hidden, d_preact)


def body(tokens, d_output, combine, routes, gate_weight, up_weight, down_weight):
    experts = lax.axis_size("expert")
    tok_count = tokens.shape[0]
    model_width = tokens.shape[1]
    top_count = routes.shape[1]
    capacity = max(2, (9 * tok_count * top_count + 8 * experts - 1) // (8 * experts))
    slot_count = experts * capacity
    slot_index = route_slots(routes, experts)
    position = (routes * capacity + slot_index).reshape(-1)
    spread_inputs = jnp.repeat(tokens, top_count, axis=0)
    scaled = (
        (combine[:, :, None] * d_output[:, None, :].astype(jnp.float32))
        .astype(jnp.bfloat16)
        .reshape(-1, model_width)
    )
    send_inputs = (
        jnp.zeros((slot_count, model_width), jnp.bfloat16)
        .at[position]
        .set(spread_inputs)
        .reshape(experts, capacity, model_width)
    )
    send_grads = (
        jnp.zeros((slot_count, model_width), jnp.bfloat16)
        .at[position]
        .set(scaled)
        .reshape(experts, capacity, model_width)
    )
    whole_gate, whole_up, whole_down = (
        lax.all_gather(gate_weight, "dp", axis=1, tiled=True),
        lax.all_gather(up_weight, "dp", axis=1, tiled=True),
        lax.all_gather(down_weight, "dp", axis=2, tiled=True),
    )
    gate_up = jnp.concatenate([whole_gate[0], whole_up[0]], axis=1)
    down_matrix = whole_down[0]
    hidden_units = down_matrix.shape[0]
    recv_inputs, recv_grads = (
        lax.all_to_all(send_inputs, "expert", split_axis=0, concat_axis=0, tiled=True),
        lax.all_to_all(send_grads, "expert", split_axis=0, concat_axis=0, tiled=True),
    )
    flat_inputs = recv_inputs.reshape(-1, model_width)
    flat_grads = recv_grads.reshape(-1, model_width)
    d_rows, hidden, d_preact = row_work(flat_inputs, flat_grads, gate_up, down_matrix)
    returned = lax.all_to_all(
        d_rows.reshape(experts, capacity, model_width),
        "expert",
        split_axis=0,
        concat_axis=0,
        tiled=True,
    )
    route_rows = returned.reshape(-1, model_width)[position].reshape(
        tok_count, top_count, model_width
    )
    d_tokens = jnp.sum(route_rows.astype(jnp.float32), axis=1).astype(jnp.bfloat16)
    gate_up_grad = jnp.dot(flat_inputs.T, d_preact, preferred_element_type=jnp.float32)
    down_grad = jnp.dot(flat_grads.T, hidden, preferred_element_type=jnp.float32)
    stacked = jnp.concatenate([gate_up_grad, down_grad], axis=1)
    summed = lax.psum_scatter(
        stacked.astype(jnp.bfloat16), "dp", scatter_dimension=0, tiled=True
    ).astype(jnp.float32)
    d_gate_weight = summed[:, :hidden_units][None]
    d_up_weight = summed[:, hidden_units : 2 * hidden_units][None]
    d_down_weight = summed[:, 2 * hidden_units :].T[None]
    return (d_tokens, d_gate_weight, d_up_weight, d_down_weight)


def solution(mesh):
    placed = (
        P(("dp", "expert"), None),
        P(("dp", "expert"), None),
        P(("dp", "expert"), None),
        P(("dp", "expert"), None),
        P("expert", "dp", None),
        P("expert", "dp", None),
        P("expert", None, "dp"),
    )
    return jax.shard_map(
        body,
        mesh=mesh,
        in_specs=placed,
        out_specs=(
            P(("dp", "expert"), None),
            P("expert", "dp", None),
            P("expert", "dp", None),
            P("expert", None, "dp"),
        ),
        check_vma=False,
    )
```

profile of v0, /device:TPU:1, one launch (start us, length us, event | category | flops | bytes accessed | tf_op | source)
XLA Modules:
  0.0 330.5 jit_solution(18078661174576874476)
XLA Ops:
  7.2 0.8 convert_reduce_fusion
  8.3 0.7 select_reduce_fusion
  10.0 6.0 %scatter_custom_fusion.1 = bf16[1152,1024]{1,0:T(8,128)(2,1)S(1)} fusion(s32[1024]{0:T(1024)S(1)} %bitcast.37, bf16[]{:T(256)} %constant.5.clone.1, bf16[128,1024]{1,0:T(8,128)(2,1)S(1)} %copy-done), kind=kCustom, calls=%fused_computation.9 | custom fusion | bytes 2621442 | tf_op jit(solution)/shard_map/scatter | solution.py:49
  16.0 2.4 reshape.84
  18.4 11.8 %all-to-all-start.1 = ((bf16[64,18,1024]{2,1,0:T(8,128)(2,1)}), bf16[64,18,1024]{2,1,0:T(8,128)(2,1)S(1)}, u32[]{:S(2)}, u32[]{:S(2)}) async-start(bf16[64,18,1024]{2,1,0:T(8,128)(2,1)} %reshape.84), calls=%async_computation.1 | async-start | bytes 6291456 | tf_op jit(solution)/shard_map/all_to_all | solution.py:67
  30.4 1.8 convert_element_type.25
  32.2 7.7 %scatter_custom_fusion = bf16[1152,1024]{1,0:T(8,128)(2,1)} fusion(s32[1024]{0:T(1024)S(1)} %bitcast.38, f32[128,1024]{1,0:T(8,128)} %convert_element_type.25, f32[1024]{0:T(1024)S(1)} %mul.60, bf16[]{:T(256)} %constant.5.clone.1), kind=kCustom, calls=%fused_computation.7 | custom fusion | flops 2097152 | bytes 2887682 | tf_op jit(solution)/shard_map/scatter | solution.py:55
  39.9 4.3 %reshape.81 = bf16[64,18,1024]{2,1,0:T(8,128)(2,1)} reshape(bf16[1152,1024]{1,0:T(8,128)(2,1)} %scatter_custom_fusion) | data formatting | bytes 4718592 | tf_op jit(solution)/shard_map/reshape | solution.py:56
  44.2 59.5 %all-to-all-done.1 = bf16[64,18,1024]{2,1,0:T(8,128)(2,1)S(1)} async-done(((bf16[64,18,1024]{2,1,0:T(8,128)(2,1)}), bf16[64,18,1024]{2,1,0:T(8,128)(2,1)S(1)}, u32[]{:S(2)}, u32[]{:S(2)}) %all-to-all-start.1) | async-done | bytes 2359328 | tf_op jit(solution)/shard_map/all_to_all | solution.py:67
  103.7 6.2 %all-to-all-start = ((bf16[64,18,1024]{2,1,0:T(8,128)(2,1)}), bf16[64,18,1024]{2,1,0:T(8,128)(2,1)}, u32[]{:S(2)}, u32[]{:S(2)}) async-start(bf16[64,18,1024]{2,1,0:T(8,128)(2,1)} %reshape.81), calls=%async_computation | async-start | bytes 6291456 | tf_op jit(solution)/shard_map/all_to_all | solution.py:68
  109.9 30.3 %all_gather.10 = bf16[1,1024,384]{2,1,0:T(8,128)(2,1)} all-gather(bf16[1,128,384]{2,1,0:T(8,128)(2,1)S(1)} %copy-done.5), channel_id=1, replica_groups=mesh['dp'=8,'expert'=64] {'dp'}, dimensions={1}, use_global_device_ids=true | all-gather | bytes 884736 | tf_op jit(solution)/shard_map/all_gather | solution.py:59
  140.2 24.1 %all_gather.11 = bf16[1,1024,384]{2,1,0:T(8,128)(2,1)} all-gather(bf16[1,128,384]{2,1,0:T(8,128)(2,1)} %param.12), channel_id=1, replica_groups=mesh['dp'=8,'expert'=64] {'dp'}, dimensions={1}, use_global_device_ids=true | all-gather | bytes 884736 | tf_op jit(solution)/shard_map/all_gather | solution.py:60
  164.3 22.5 %all_gather.9 = bf16[1,384,1024]{2,1,0:T(8,128)(2,1)} all-gather(bf16[1,384,128]{2,1,0:T(8,128)(2,1)} %param.13), channel_id=1, replica_groups=mesh['dp'=8,'expert'=64] {'dp'}, dimensions={2}, use_global_device_ids=true | all-gather | bytes 884736 | tf_op jit(solution)/shard_map/all_gather | solution.py:61
  186.8 2.2 reshape.85
  189.0 6.1 %fusion.10 = f32[1152,768]{0,1:T(8,128)} fusion(bf16[1152,1024]{1,0:T(8,128)(2,1)} %reshape.85, bf16[1024,384]{1,0:T(8,128)(2,1)} %bitcast.35, bf16[1024,384]{1,0:T(8,128)(2,1)} %bitcast.33), kind=kOutput, calls=%fused_computation.24 | convolution fusion | flops 1815085056 | bytes 7471104 | tf_op jit(solution)/shard_map/dot_general | solution.py:18
  195.1 2.9 reshape.82
  198.1 3.4 %convolution_convert_fusion.2 = bf16[1024,384]{0,1:T(8,128)(2,1)S(1)} fusion(bf16[1152,1024]{1,0:T(8,128)(2,1)S(1)} %reshape.82, f32[1152,768]{0,1:T(8,128)} %fusion.10), kind=kOutput, calls=%fused_computation.20 | convolution fusion | flops 909017088 | bytes 6684672 | tf_op jit(solution)/shard_map/dot_general | solution.py:85
  201.5 1.6 multiply_convert_fusion.2
  203.2 3.3 %convolution_convert_fusion.1 = bf16[1024,768]{0,1:T(8,128)(2,1)} fusion(bf16[1152,1024]{1,0:T(8,128)(2,1)S(1)} %copy-done.1, bf16[1152,384]{0,1:T(8,128)(2,1)S(1)} %get-tuple-element.21, bf16[1152,384]{0,1:T(8,128)(2,1)S(1)} %get-tuple-element.20), kind=kOutput, calls=%fused_computation.18 | convolution fusion | flops 1816264704 | bytes 5701632 | tf_op jit(solution)/shard_map/dot_general | solution.py:84
  206.5 2.1 convolution_convert_fusion
  208.6 2.5 reshape.86
  211.0 23.6 %all-to-all-start.2 = ((bf16[64,18,1024]{2,1,0:T(8,128)(2,1)}), bf16[64,18,1024]{2,1,0:T(8,128)(2,1)}, u32[]{:S(2)}, u32[]{:S(2)}) async-start(bf16[64,18,1024]{2,1,0:T(8,128)(2,1)} %reshape.86), calls=%async_computation.2 | async-start | bytes 6291456 | tf_op jit(solution)/shard_map/all_to_all | solution.py:73
  234.9 1.6 pad_maximum_fusion
  236.5 2.5 copy.31
  239.1 69.0 %all-to-all-done.2 = bf16[64,18,1024]{2,1,0:T(8,128)(2,1)} async-done(((bf16[64,18,1024]{2,1,0:T(8,128)(2,1)}), bf16[64,18,1024]{2,1,0:T(8,128)(2,1)}, u32[]{:S(2)}, u32[]{:S(2)}) %all-to-all-start.2) | async-done | bytes 2359328 | tf_op jit(solution)/shard_map/all_to_all | solution.py:73
  308.1 2.9 reshape.87
  311.0 5.4 %gather_fusion = bf16[1024,1024]{1,0:T(8,128)(2,1)} fusion(bf16[1152,1024]{1,0:T(8,128)(2,1)S(1)} %reshape.87, s32[1024]{0:T(1024)S(1)} %broadcast_clamp_fusion), kind=kCustom, calls=%fused_computation | custom fusion | bytes 4198400 | tf_op jit(solution)/shard_map/gather | solution.py:80
  316.4 3.7 %bitcast_reduce_fusion = bf16[128,1024]{1,0:T(8,128)(2,1)} fusion(bf16[1024,1024]{1,0:T(8,128)(2,1)} %gather_fusion), kind=kLoop, calls=%fused_computation.8 | loop fusion | flops 917504 | bytes 2359296 | tf_op jit(solution)/shard_map/reduce_sum | solution.py:83
  320.1 1.2 copy.32
  321.3 0.7 slice_bitcast_fusion
  322.1 0.8 copy.30
  322.9 0.8 copy.29
  (32 shorter events, 1.8 us)
Async XLA Ops:
  7.2 2.8 copy-start
  18.4 11.8 %copy-start.6 = (f32[128,8]{0,1:T(8,128)S(1)}, f32[128,8]{0,1:T(8,128)}, u32[]{:S(2)}) copy-start(f32[128,8]{0,1:T(8,128)} %param.9) | copy-start | bytes 12292
  18.4 85.3 %all-to-all-start.1 = ((bf16[64,18,1024]{2,1,0:T(8,128)(2,1)}), bf16[64,18,1024]{2,1,0:T(8,128)(2,1)S(1)}, u32[]{:S(2)}, u32[]{:S(2)}) async-start(bf16[64,18,1024]{2,1,0:T(8,128)(2,1)} %reshape.84), calls=%async_computation.1 | async-start | bytes 6291456 | tf_op jit(solution)/shard_map/all_to_all | solution.py:67
  44.2 65.8 %copy-start.5 = (bf16[1,128,384]{2,1,0:T(8,128)(2,1)S(1)}, bf16[1,128,384]{2,1,0:T(8,128)(2,1)}, u32[]{:S(2)}) copy-start(bf16[1,128,384]{2,1,0:T(8,128)(2,1)} %param.11) | copy-start | bytes 294916
  103.7 91.5 %all-to-all-start = ((bf16[64,18,1024]{2,1,0:T(8,128)(2,1)}), bf16[64,18,1024]{2,1,0:T(8,128)(2,1)}, u32[]{:S(2)}, u32[]{:S(2)}) async-start(bf16[64,18,1024]{2,1,0:T(8,128)(2,1)} %reshape.81), calls=%async_computation | async-start | bytes 6291456 | tf_op jit(solution)/shard_map/all_to_all | solution.py:68
  198.1 3.4 %copy-start.4 = (bf16[1,384,1024]{2,1,0:T(8,128)(2,1)S(1)}, bf16[1,384,1024]{2,1,0:T(8,128)(2,1)}, u32[]{:S(2)}) copy-start(bf16[1,384,1024]{2,1,0:T(8,128)(2,1)} %all_gather.9) | copy-start | bytes 2359300
  198.1 3.4 %copy-start.7 = (f32[1152,768]{0,1:T(8,128)S(1)}, f32[1152,768]{0,1:T(8,128)}, u32[]{:S(2)}) copy-start(f32[1152,768]{0,1:T(8,128)} %fusion.10) | copy-start | bytes 10616836
  201.5 1.7 copy-start.1
  203.1 3.3 %copy-start.2 = (bf16[1,1024,384]{2,1,0:T(8,128)(2,1)S(1)}, bf16[1,1024,384]{2,1,0:T(8,128)(2,1)}, u32[]{:S(2)}) copy-start(bf16[1,1024,384]{2,1,0:T(8,128)(2,1)} %all_gather.10) | copy-start | bytes 2359300
  203.1 3.3 %copy-start.3 = (bf16[1,1024,384]{2,1,0:T(8,128)(2,1)S(1)}, bf16[1,1024,384]{2,1,0:T(8,128)(2,1)}, u32[]{:S(2)}) copy-start(bf16[1,1024,384]{2,1,0:T(8,128)(2,1)} %all_gather.11) | copy-start | bytes 2359300
  211.0 97.1 %all-to-all-start.2 = ((bf16[64,18,1024]{2,1,0:T(8,128)(2,1)}), bf16[64,18,1024]{2,1,0:T(8,128)(2,1)}, u32[]{:S(2)}, u32[]{:S(2)}) async-start(bf16[64,18,1024]{2,1,0:T(8,128)(2,1)} %reshape.86), calls=%async_computation.2 | async-start | bytes 6291456 | tf_op jit(solution)/shard_map/all_to_all | solution.py:73
  234.7 85.5 %reduce-scatter.4.cloned.1.call-start = ((), (), s32[]{:S(2)}) async-start(), calls=%async_computation.4 | async-start | bytes 2654208
Sparse Core Ops, SparseCore 0:
  239.2 41.3 reduce-scatter.3
where the time goes:
time: 331 us
  waiting for transfers between devices  129 us (39%)
  blocking collectives  76.9 us (23%)
  starting transfers between devices  41.9 us (13%)
  local copies, waits for them, and re-layouts  35.3 us (11%)
  other arithmetic  17.3 us (5%)
  matrix products  16.5 us (5%)
  between operations  14.2 us (4%)
    all_to_all x1, waiting for transfers between devices, body(): lax.all_to_all(d_rows.reshape(experts, capacity, model_width), 'expert',...  69 us
    all_to_all x1, waiting for transfers between devices, body(): lax.all_to_all(send_inputs, 'expert', split_axis=0, concat_axis=0, tiled=...  59.5 us
    all_gather x1, blocking collectives, body(): lax.all_gather(gate_weight, 'dp', axis=1, tiled=True)  30.3 us
    all_gather x1, blocking collectives, body(): lax.all_gather(up_weight, 'dp', axis=1, tiled=True)  24.1 us
    all_to_all x1, starting transfers between devices, body(): lax.all_to_all(d_rows.reshape(experts, capacity, model_width), 'expert',...  23.6 us
    all_gather x1, blocking collectives, body(): lax.all_gather(down_weight, 'dp', axis=2, tiled=True)  22.5 us
    all_to_all x1, starting transfers between devices, body(): lax.all_to_all(send_inputs, 'expert', split_axis=0, concat_axis=0, tiled=...  11.8 us
    scatter x1, other arithmetic, body(): send_grads = jnp.zeros((slot_count, model_width), jnp.bfloat16).at[positi...  7.71 us
  transfers between devices with their start and end apart: 4, of which 2 were waited for; matrix products, arithmetic and copies ran while one was open for 12% of the time, Pallas kernels for 0%

commit v1 on v0

--- a/solution.py
+++ b/solution.py
@@ -9,7 +9,11 @@
         jnp.int32
     )
     per_token = jnp.sum(matches, axis=1)
-    earlier = jnp.cumsum(per_token, axis=0) - per_token
+    tok_count = per_token.shape[0]
+    before = jnp.tri(tok_count, k=-1, dtype=jnp.bfloat16)
+    earlier = jnp.dot(
+        before, per_token.astype(jnp.bfloat16), preferred_element_type=jnp.float32
+    ).astype(jnp.int32)
     return jnp.sum(matches * earlier[:, None, :], axis=2)
 
 

time: 331 us -> 331 us (level)
  no operation moved by 1% of the time
where the time goes in v1:
time: 331 us; the launch traced here: 330 us
  waiting for transfers between devices  128 us (39%)
  blocking collectives  76.9 us (23%)
  starting transfers between devices  41.9 us (13%)
  local copies, waits for them, and re-layouts  35.2 us (11%)
  other arithmetic  17.1 us (5%)
  matrix products  16.7 us (5%)
  between operations  14.2 us (4%)
    all_to_all x1, waiting for transfers between devices, body(): lax.all_to_all(d_rows.reshape(experts, capacity, model_width), 'expert',...  68.9 us
    all_to_all x1, waiting for transfers between devices, body(): lax.all_to_all(send_inputs, 'expert', split_axis=0, concat_axis=0, tiled=...  59.5 us
    all_gather x1, blocking collectives, body(): lax.all_gather(gate_weight, 'dp', axis=1, tiled=True)  30.3 us
    all_gather x1, blocking collectives, body(): lax.all_gather(up_weight, 'dp', axis=1, tiled=True)  24.1 us
    all_to_all x1, starting transfers between devices, body(): lax.all_to_all(d_rows.reshape(experts, capacity, model_width), 'expert',...  23.6 us
    all_gather x1, blocking collectives, body(): lax.all_gather(down_weight, 'dp', axis=2, tiled=True)  22.5 us
    all_to_all x1, starting transfers between devices, body(): lax.all_to_all(send_inputs, 'expert', split_axis=0, concat_axis=0, tiled=...  11.8 us
    scatter x1, other arithmetic, body(): send_grads = jnp.zeros((slot_count, model_width), jnp.bfloat16).at[positi...  7.72 us
  transfers between devices with their start and end apart: 4, of which 2 were waited for; matrix products, arithmetic and copies ran while one was open for 12% of the time, Pallas kernels for 0%

profile of v1, /device:TPU:1, one launch (start us, length us, event | category | flops | bytes accessed | tf_op | source)
XLA Modules:
  0.0 330.3 jit_solution(3674698657693354905)
XLA Ops:
  7.2 0.8 convert_reduce_fusion
  8.2 0.7 select_reduce_fusion
  9.8 6.0 %scatter_custom_fusion.1 = bf16[1152,1024]{1,0:T(8,128)(2,1)S(1)} fusion(s32[1024]{0:T(1024)S(1)} %bitcast.37, bf16[]{:T(256)} %constant.6.clone.1, bf16[128,1024]{1,0:T(8,128)(2,1)S(1)} %copy-done), kind=kCustom, calls=%fused_computation.9 | custom fusion | bytes 2621442 | tf_op jit(solution)/shard_map/scatter | solution.py:53
  15.9 2.4 reshape.76
  18.3 11.8 %all-to-all-start.1 = ((bf16[64,18,1024]{2,1,0:T(8,128)(2,1)}), bf16[64,18,1024]{2,1,0:T(8,128)(2,1)S(1)}, u32[]{:S(2)}, u32[]{:S(2)}) async-start(bf16[64,18,1024]{2,1,0:T(8,128)(2,1)} %reshape.76), calls=%async_computation.1 | async-start | bytes 6291456 | tf_op jit(solution)/shard_map/all_to_all | solution.py:71
  30.2 1.8 convert_element_type.34
  32.0 7.7 %scatter_custom_fusion = bf16[1152,1024]{1,0:T(8,128)(2,1)} fusion(s32[1024]{0:T(1024)S(1)} %bitcast.38, f32[128,1024]{1,0:T(8,128)} %convert_element_type.34, f32[1024]{0:T(1024)S(1)} %mul.60, bf16[]{:T(256)} %constant.6.clone.1), kind=kCustom, calls=%fused_computation.7 | custom fusion | flops 2097152 | bytes 2887682 | tf_op jit(solution)/shard_map/scatter | solution.py:59
  39.7 4.3 %reshape.73 = bf16[64,18,1024]{2,1,0:T(8,128)(2,1)} reshape(bf16[1152,1024]{1,0:T(8,128)(2,1)} %scatter_custom_fusion) | data formatting | bytes 4718592 | tf_op jit(solution)/shard_map/reshape | solution.py:60
  44.1 59.5 %all-to-all-done.1 = bf16[64,18,1024]{2,1,0:T(8,128)(2,1)S(1)} async-done(((bf16[64,18,1024]{2,1,0:T(8,128)(2,1)}), bf16[64,18,1024]{2,1,0:T(8,128)(2,1)S(1)}, u32[]{:S(2)}, u32[]{:S(2)}) %all-to-all-start.1) | async-done | bytes 2359328 | tf_op jit(solution)/shard_map/all_to_all | solution.py:71
  103.5 6.2 %all-to-all-start = ((bf16[64,18,1024]{2,1,0:T(8,128)(2,1)}), bf16[64,18,1024]{2,1,0:T(8,128)(2,1)}, u32[]{:S(2)}, u32[]{:S(2)}) async-start(bf16[64,18,1024]{2,1,0:T(8,128)(2,1)} %reshape.73), calls=%async_computation | async-start | bytes 6291456 | tf_op jit(solution)/shard_map/all_to_all | solution.py:72
  109.8 30.3 %all_gather.10 = bf16[1,1024,384]{2,1,0:T(8,128)(2,1)} all-gather(bf16[1,128,384]{2,1,0:T(8,128)(2,1)S(1)} %copy-done.5), channel_id=1, replica_groups=mesh['dp'=8,'expert'=64] {'dp'}, dimensions={1}, use_global_device_ids=true | all-gather | bytes 884736 | tf_op jit(solution)/shard_map/all_gather | solution.py:63
  140.1 24.1 %all_gather.11 = bf16[1,1024,384]{2,1,0:T(8,128)(2,1)} all-gather(bf16[1,128,384]{2,1,0:T(8,128)(2,1)} %param.12), channel_id=1, replica_groups=mesh['dp'=8,'expert'=64] {'dp'}, dimensions={1}, use_global_device_ids=true | all-gather | bytes 884736 | tf_op jit(solution)/shard_map/all_gather | solution.py:64
  164.2 22.5 %all_gather.9 = bf16[1,384,1024]{2,1,0:T(8,128)(2,1)} all-gather(bf16[1,384,128]{2,1,0:T(8,128)(2,1)} %param.13), channel_id=1, replica_groups=mesh['dp'=8,'expert'=64] {'dp'}, dimensions={2}, use_global_device_ids=true | all-gather | bytes 884736 | tf_op jit(solution)/shard_map/all_gather | solution.py:65
  186.7 2.2 reshape.77
  188.9 6.1 %fusion.10 = f32[1152,768]{0,1:T(8,128)} fusion(bf16[1152,1024]{1,0:T(8,128)(2,1)} %reshape.77, bf16[1024,384]{1,0:T(8,128)(2,1)} %bitcast.35, bf16[1024,384]{1,0:T(8,128)(2,1)} %bitcast.33), kind=kOutput, calls=%fused_computation.25 | convolution fusion | flops 1815085056 | bytes 7471104 | tf_op jit(solution)/shard_map/dot_general | solution.py:22
  195.0 2.9 reshape.74
  197.9 3.4 %convolution_convert_fusion.2 = bf16[1024,384]{0,1:T(8,128)(2,1)S(1)} fusion(bf16[1152,1024]{1,0:T(8,128)(2,1)S(1)} %reshape.74, f32[1152,768]{0,1:T(8,128)} %fusion.10), kind=kOutput, calls=%fused_computation.20 | convolution fusion | flops 909017088 | bytes 6684672 | tf_op jit(solution)/shard_map/dot_general | solution.py:89
  201.4 1.6 multiply_convert_fusion.2
  203.0 3.3 %convolution_convert_fusion.1 = bf16[1024,768]{0,1:T(8,128)(2,1)} fusion(bf16[1152,1024]{1,0:T(8,128)(2,1)S(1)} %copy-done.1, bf16[1152,384]{0,1:T(8,128)(2,1)S(1)} %get-tuple-element.21, bf16[1152,384]{0,1:T(8,128)(2,1)S(1)} %get-tuple-element.20), kind=kOutput, calls=%fused_computation.18 | convolution fusion | flops 1816264704 | bytes 5701632 | tf_op jit(solution)/shard_map/dot_general | solution.py:88
  206.4 2.1 convolution_convert_fusion
  208.5 2.4 reshape.78
  210.9 23.6 %all-to-all-start.2 = ((bf16[64,18,1024]{2,1,0:T(8,128)(2,1)}), bf16[64,18,1024]{2,1,0:T(8,128)(2,1)}, u32[]{:S(2)}, u32[]{:S(2)}) async-start(bf16[64,18,1024]{2,1,0:T(8,128)(2,1)} %reshape.78), calls=%async_computation.2 | async-start | bytes 6291456 | tf_op jit(solution)/shard_map/all_to_all | solution.py:77
  234.8 1.6 pad_maximum_fusion
  236.4 2.6 copy.31
  239.0 68.9 %all-to-all-done.2 = bf16[64,18,1024]{2,1,0:T(8,128)(2,1)} async-done(((bf16[64,18,1024]{2,1,0:T(8,128)(2,1)}), bf16[64,18,1024]{2,1,0:T(8,128)(2,1)}, u32[]{:S(2)}, u32[]{:S(2)}) %all-to-all-start.2) | async-done | bytes 2359328 | tf_op jit(solution)/shard_map/all_to_all | solution.py:77
  307.9 2.9 reshape.79
  310.9 5.3 %gather_fusion = bf16[1024,1024]{1,0:T(8,128)(2,1)} fusion(bf16[1152,1024]{1,0:T(8,128)(2,1)S(1)} %reshape.79, s32[1024]{0:T(1024)S(1)} %broadcast_clamp_fusion), kind=kCustom, calls=%fused_computation | custom fusion | bytes 4198400 | tf_op jit(solution)/shard_map/gather | solution.py:84
  316.2 3.7 %bitcast_reduce_fusion = bf16[128,1024]{1,0:T(8,128)(2,1)} fusion(bf16[1024,1024]{1,0:T(8,128)(2,1)} %gather_fusion), kind=kLoop, calls=%fused_computation.8 | loop fusion | flops 917504 | bytes 2359296 | tf_op jit(solution)/shard_map/reduce_sum | solution.py:87
  319.9 1.2 copy.32
  321.2 0.7 slice_bitcast_fusion
  321.9 0.8 copy.30
  322.7 0.8 copy.29
  (30 shorter events, 1.7 us)
Async XLA Ops:
  7.2 2.7 copy-start
  18.3 11.8 %copy-start.6 = (f32[128,8]{0,1:T(8,128)S(1)}, f32[128,8]{0,1:T(8,128)}, u32[]{:S(2)}) copy-start(f32[128,8]{0,1:T(8,128)} %param.9) | copy-start | bytes 12292
  18.3 85.3 %all-to-all-start.1 = ((bf16[64,18,1024]{2,1,0:T(8,128)(2,1)}), bf16[64,18,1024]{2,1,0:T(8,128)(2,1)S(1)}, u32[]{:S(2)}, u32[]{:S(2)}) async-start(bf16[64,18,1024]{2,1,0:T(8,128)(2,1)} %reshape.76), calls=%async_computation.1 | async-start | bytes 6291456 | tf_op jit(solution)/shard_map/all_to_all | solution.py:71
  44.1 65.7 %copy-start.5 = (bf16[1,128,384]{2,1,0:T(8,128)(2,1)S(1)}, bf16[1,128,384]{2,1,0:T(8,128)(2,1)}, u32[]{:S(2)}) copy-start(bf16[1,128,384]{2,1,0:T(8,128)(2,1)} %param.11) | copy-start | bytes 294916
  103.5 91.4 %all-to-all-start = ((bf16[64,18,1024]{2,1,0:T(8,128)(2,1)}), bf16[64,18,1024]{2,1,0:T(8,128)(2,1)}, u32[]{:S(2)}, u32[]{:S(2)}) async-start(bf16[64,18,1024]{2,1,0:T(8,128)(2,1)} %reshape.73), calls=%async_computation | async-start | bytes 6291456 | tf_op jit(solution)/shard_map/all_to_all | solution.py:72
  197.9 3.4 %copy-start.4 = (bf16[1,384,1024]{2,1,0:T(8,128)(2,1)S(1)}, bf16[1,384,1024]{2,1,0:T(8,128)(2,1)}, u32[]{:S(2)}) copy-start(bf16[1,384,1024]{2,1,0:T(8,128)(2,1)} %all_gather.9) | copy-start | bytes 2359300
  197.9 3.4 %copy-start.7 = (f32[1152,768]{0,1:T(8,128)S(1)}, f32[1152,768]{0,1:T(8,128)}, u32[]{:S(2)}) copy-start(f32[1152,768]{0,1:T(8,128)} %fusion.10) | copy-start | bytes 10616836
  201.4 1.7 copy-start.1
  203.0 3.4 %copy-start.2 = (bf16[1,1024,384]{2,1,0:T(8,128)(2,1)S(1)}, bf16[1,1024,384]{2,1,0:T(8,128)(2,1)}, u32[]{:S(2)}) copy-start(bf16[1,1024,384]{2,1,0:T(8,128)(2,1)} %all_gather.10) | copy-start | bytes 2359300
  203.0 3.4 %copy-start.3 = (bf16[1,1024,384]{2,1,0:T(8,128)(2,1)S(1)}, bf16[1,1024,384]{2,1,0:T(8,128)(2,1)}, u32[]{:S(2)}) copy-start(bf16[1,1024,384]{2,1,0:T(8,128)(2,1)} %all_gather.11) | copy-start | bytes 2359300
  210.9 97.1 %all-to-all-start.2 = ((bf16[64,18,1024]{2,1,0:T(8,128)(2,1)}), bf16[64,18,1024]{2,1,0:T(8,128)(2,1)}, u32[]{:S(2)}, u32[]{:S(2)}) async-start(bf16[64,18,1024]{2,1,0:T(8,128)(2,1)} %reshape.78), calls=%async_computation.2 | async-start | bytes 6291456 | tf_op jit(solution)/shard_map/all_to_all | solution.py:77
  234.5 85.5 %reduce-scatter.4.cloned.1.call-start = ((), (), s32[]{:S(2)}) async-start(), calls=%async_computation.4 | async-start | bytes 2654208
Sparse Core Ops, SparseCore 0:
  239.1 41.3 reduce-scatter.3

commit v2 on v0

v2 whole, which is shorter than its diff:
```python
import jax
import jax.numpy as jnp
from jax import lax
from jax.sharding import PartitionSpec as P


def slot_map(routes, combine, experts, capacity):
    tok_count = routes.shape[0]
    ids = jnp.arange(experts, dtype=jnp.int32)[:, None, None]
    matches = routes.T[None, :, :] == ids
    member = jnp.any(matches, axis=1)
    scale = jnp.sum(jnp.where(matches, combine.T[None], 0.0), axis=1)
    before = jnp.triu(jnp.ones((tok_count, tok_count), jnp.bfloat16), k=1)
    rank = jnp.dot(
        member.astype(jnp.bfloat16), before, preferred_element_type=jnp.float32
    ).astype(jnp.int32)
    slots = jnp.arange(capacity, dtype=jnp.int32)[None, :, None]
    pick = (rank[:, None, :] == slots) & member[:, None, :]
    slot_scale = jnp.sum(jnp.where(pick, scale[:, None, :], 0.0), axis=2)
    return pick.astype(jnp.bfloat16), slot_scale


def row_work(row_inputs, row_grads, gate_up, down_t):
    hidden_units = down_t.shape[1]
    preact = jnp.dot(row_inputs, gate_up, preferred_element_type=jnp.float32)
    gate_pre = preact[:, :hidden_units]
    up_pre = preact[:, hidden_units:]
    gate_sigmoid = jax.nn.sigmoid(gate_pre)
    hidden = (gate_pre * gate_sigmoid * up_pre).astype(jnp.bfloat16)
    d_hidden = jnp.dot(row_grads, down_t, preferred_element_type=jnp.float32)
    d_gate_pre = d_hidden * up_pre * gate_sigmoid * (1.0 + gate_pre * (1.0 - gate_sigmoid))
    d_up_pre = d_hidden * gate_pre * gate_sigmoid
    d_preact = jnp.concatenate([d_gate_pre, d_up_pre], axis=1).astype(jnp.bfloat16)
    d_rows = jnp.dot(d_preact, gate_up.T, preferred_element_type=jnp.float32).astype(jnp.bfloat16)
    return (d_rows, hidden, d_preact)


def body(tokens, d_output, combine, routes, gate_weight, up_weight, down_weight):
    experts = lax.axis_size("expert")
    tok_count = tokens.shape[0]
    model_width = tokens.shape[1]
    hidden_units = gate_weight.shape[2]
    top_count = routes.shape[1]
    capacity = max(2, (9 * tok_count * top_count + 8 * experts - 1) // (8 * experts))
    mine = jnp.concatenate([gate_weight[0], up_weight[0], down_weight[0].T], axis=1)
    whole = lax.all_gather(mine, "dp", axis=0, tiled=True)
    pick, slot_scale = slot_map(routes, combine, experts, capacity)
    send_inputs = jnp.einsum(
        "ect,td->ecd", pick, tokens, preferred_element_type=jnp.float32
    ).astype(jnp.bfloat16)
    send_grads = (
        slot_scale[:, :, None]
        * jnp.einsum("ect,td->ecd", pick, d_output, preferred_element_type=jnp.float32)
    ).astype(jnp.bfloat16)
    recv_inputs, recv_grads = (
        lax.all_to_all(send_inputs, "expert", split_axis=0, concat_axis=0, tiled=True),
        lax.all_to_all(send_grads, "expert", split_axis=0, concat_axis=0, tiled=True),
    )
    flat_inputs = recv_inputs.reshape(-1, model_width)
    flat_grads = recv_grads.reshape(-1, model_width)
    gate_up = whole[:, : 2 * hidden_units]
    down_t = whole[:, 2 * hidden_units :]
    d_rows, hidden, d_preact = row_work(flat_inputs, flat_grads, gate_up, down_t)
    returned = lax.all_to_all(
        d_rows.reshape(experts, capacity, model_width),
        "expert",
        split_axis=0,
        concat_axis=0,
        tiled=True,
    )
    d_tokens = jnp.einsum(
        "ect,ecd->td", pick, returned, preferred_element_type=jnp.float32
    ).astype(jnp.bfloat16)
    gate_up_grad = jnp.dot(flat_inputs.T, d_preact, preferred_element_type=jnp.float32)
    down_grad = jnp.dot(flat_grads.T, hidden, preferred_element_type=jnp.float32)
    stacked = jnp.concatenate([gate_up_grad, down_grad], axis=1)
    summed = lax.psum_scatter(
        stacked.astype(jnp.bfloat16), "dp", scatter_dimension=0, tiled=True
    ).astype(jnp.float32)
    d_gate_weight = summed[:, :hidden_units][None]
    d_up_weight = summed[:, hidden_units : 2 * hidden_units][None]
    d_down_weight = summed[:, 2 * hidden_units :].T[None]
    return (d_tokens, d_gate_weight, d_up_weight, d_down_weight)


def solution(mesh):
    placed = (
        P(("dp", "expert"), None),
        P(("dp", "expert"), None),
        P(("dp", "expert"), None),
        P(("dp", "expert"), None),
        P("expert", "dp", None),
        P("expert", "dp", None),
        P("expert", None, "dp"),
    )
    return jax.shard_map(
        body,
        mesh=mesh,
        in_specs=placed,
        out_specs=(
            P(("dp", "expert"), None),
            P("expert", "dp", None),
            P("expert", "dp", None),
            P("expert", None, "dp"),
        ),
        check_vma=False,
    )
```

time: 331 us -> 294 us (0.89)
  blocking collectives: 76.9 us -> 0 us
  waiting for transfers between devices: 129 us -> 204 us
  starting transfers between devices: 41.9 us -> 24.6 us
  other arithmetic: 17.3 us -> 5.18 us
  local copies, waits for them, and re-layouts: 35.3 us -> 24.3 us
  matrix products: 16.5 us -> 20.8 us
    all_gather x3 -> x0, blocking collectives: 76.9 us -> none  [the longest x1 30.3 us: body(): lax.all_gather(gate_weight, 'dp', axis=1, tiled=True)]
    all_to_all x1, waiting for transfers between devices: 0.01 us -> 68.7 us  [body(): lax.all_to_all(send_grads, 'expert', split_axis=0, concat_axis=0, tiled=T...]
    all_to_all x1, starting transfers between devices: 23.6 us -> 6.25 us  [body(): lax.all_to_all(d_rows.reshape(experts, capacity, model_width), 'expert',...]
    reshape x4 -> x0, local copies, waits for them, and re-layouts: 9.74 us -> none  [the longest x1 4.29 us: body(): send_grads = jnp.zeros((slot_count, model_width), jnp.bfloat16).at[positi...]
    dot_general x1 -> x5, matrix products: 1.63 us -> 9.58 us  [the longest x1 5.34 us: body(): jnp.einsum('ect,ecd->td', pick, returned, preferred_element_type=jnp.floa...]
    scatter x1 -> x0, other arithmetic: 7.71 us -> none  [body(): send_grads = jnp.zeros((slot_count, model_width), jnp.bfloat16).at[positi...]
    all_to_all x1, waiting for transfers between devices: 59.5 us -> 66.5 us  [body(): lax.all_to_all(send_inputs, 'expert', split_axis=0, concat_axis=0, tiled=...]
    convert_element_type x0 -> x2, local copies, waits for them, and re-layouts: none -> 6.09 us  [the longest x1 3.06 us: body(): send_inputs = jnp.einsum('ect,td->ecd', pick, tokens, preferred_element_t...]
  transfers between devices with their start and end apart: 4 -> 5, of which waited for: 2 -> 3; matrix products, arithmetic and copies ran while one was open for 12% -> 9% of each run, Pallas kernels for 0% -> 0%
where the time goes in v2:
time: 294 us; the launch traced here: 293 us
  waiting for transfers between devices  204 us (69%)
  starting transfers between devices  24.6 us (8%)
  local copies, waits for them, and re-layouts  24.3 us (8%)
  matrix products  20.8 us (7%)
  between operations  14.2 us (5%)
  other arithmetic  5.18 us (2%)
    all_to_all x1, waiting for transfers between devices, body(): lax.all_to_all(d_rows.reshape(experts, capacity, model_width), 'expert',...  69 us
    all_to_all x1, waiting for transfers between devices, body(): lax.all_to_all(send_grads, 'expert', split_axis=0, concat_axis=0, tiled=T...  68.7 us
    all_to_all x1, waiting for transfers between devices, body(): lax.all_to_all(send_inputs, 'expert', split_axis=0, concat_axis=0, tiled=...  66.5 us
    all_to_all x1, starting transfers between devices, body(): lax.all_to_all(send_grads, 'expert', split_axis=0, concat_axis=0, tiled=T...  11.6 us
    unnamed x14, local copies, waits for them, and re-layouts  8.41 us
    all_to_all x1, starting transfers between devices, body(): lax.all_to_all(d_rows.reshape(experts, capacity, model_width), 'expert',...  6.25 us
    all_to_all x1, starting transfers between devices, body(): lax.all_to_all(send_inputs, 'expert', split_axis=0, concat_axis=0, tiled=...  6.25 us
  transfers between devices with their start and end apart: 5, of which 3 were waited for; matrix products, arithmetic and copies ran while one was open for 9% of the time, Pallas kernels for 0%

profile of v2, /device:TPU:1, one launch (start us, length us, event | category | flops | bytes accessed | tf_op | source)
XLA Modules:
  0.0 293.2 jit_solution(16555085369447374028)
XLA Ops:
  7.2 0.8 fusion.25
  8.1 0.8 select_reduce_fusion.1
  9.2 0.8 multiply_convert_fusion
  10.0 3.0 %copy.30 = bf16[64,18,1024]{2,1,0:T(8,128)(2,1)} copy(bf16[64,18,1024]{2,0,1:T(8,128)(2,1)S(1)} %multiply_convert_fusion) | data formatting | bytes 4718592 | tf_op jit(solution)/shard_map/convert_element_type | solution.py:54
  13.0 11.6 %all-to-all-start = ((bf16[64,18,1024]{2,1,0:T(8,128)(2,1)}), bf16[64,18,1024]{2,1,0:T(8,128)(2,1)S(1)}, u32[]{:S(2)}, u32[]{:S(2)}) async-start(bf16[64,18,1024]{2,1,0:T(8,128)(2,1)} %copy.30), calls=%async_computation | async-start | bytes 6291456 | tf_op jit(solution)/shard_map/all_to_all | solution.py:57
  24.6 1.7 convolution_convert_fusion.1
  26.3 3.1 %copy.33 = bf16[64,18,1024]{2,1,0:T(8,128)(2,1)} copy(bf16[64,18,1024]{2,0,1:T(8,128)(2,1)S(1)} %convolution_convert_fusion.1) | data formatting | bytes 4718592 | tf_op jit(solution)/shard_map/convert_element_type | solution.py:50
  29.4 68.7 %all-to-all-done = bf16[64,18,1024]{2,1,0:T(8,128)(2,1)S(1)} async-done(((bf16[64,18,1024]{2,1,0:T(8,128)(2,1)}), bf16[64,18,1024]{2,1,0:T(8,128)(2,1)S(1)}, u32[]{:S(2)}, u32[]{:S(2)}) %all-to-all-start) | async-done | bytes 2359328 | tf_op jit(solution)/shard_map/all_to_all | solution.py:57
  98.1 6.2 %all-to-all-start.1 = ((bf16[64,18,1024]{2,1,0:T(8,128)(2,1)}), bf16[64,18,1024]{2,1,0:T(8,128)(2,1)}, u32[]{:S(2)}, u32[]{:S(2)}) async-start(bf16[64,18,1024]{2,1,0:T(8,128)(2,1)} %copy.33), calls=%async_computation.1 | async-start | bytes 6291456 | tf_op jit(solution)/shard_map/all_to_all | solution.py:56
  104.6 1.0 copy.31
  105.6 1.6 copy.32
  107.2 1.7 pad_maximum_fusion.4
  108.9 2.3 reshape.23
  111.3 66.5 %all-to-all-done.1 = bf16[64,18,1024]{2,1,0:T(8,128)(2,1)} async-done(((bf16[64,18,1024]{2,1,0:T(8,128)(2,1)}), bf16[64,18,1024]{2,1,0:T(8,128)(2,1)}, u32[]{:S(2)}, u32[]{:S(2)}) %all-to-all-start.1) | async-done | bytes 2359328 | tf_op jit(solution)/shard_map/all_to_all | solution.py:56
  177.8 4.3 %reshape.24 = bf16[1152,1024]{1,0:T(8,128)(2,1)} reshape(bf16[64,18,1024]{2,1,0:T(8,128)(2,1)} %all-to-all-done.1) | data formatting | bytes 4718592 | tf_op jit(solution)/shard_map/reshape | solution.py:59
  182.1 4.5 %fusion.3 = f32[1152,768]{0,1:T(8,128)S(1)} fusion(bf16[1152,1024]{1,0:T(8,128)(2,1)} %reshape.24, bf16[1024,1152]{0,1:T(8,128)(2,1)} %all-gather.2.cloned.1.call-done), kind=kOutput, calls=%fused_computation.14 | convolution fusion | flops 1811939328 | bytes 7471104 | tf_op jit(solution)/shard_map/dot_general | solution.py:25
  186.7 1.3 convolution_convert_fusion.3
  187.9 0.4 copy-done.3
  188.3 1.6 multiply_convert_fusion.3
  190.0 3.4 %convolution_convert_fusion.2 = bf16[1024,768]{0,1:T(8,128)(2,1)} fusion(bf16[1152,1024]{1,0:T(8,128)(2,1)S(1)} %copy-done.2, bf16[1152,384]{0,1:T(8,128)(2,1)S(1)} %get-tuple-element.21, bf16[1152,384]{0,1:T(8,128)(2,1)S(1)} %get-tuple-element.20), kind=kOutput, calls=%fused_computation.11 | convolution fusion | flops 1816264704 | bytes 5701632 | tf_op jit(solution)/shard_map/dot_general | solution.py:74
  193.3 2.0 convolution_convert_fusion
  195.4 2.4 reshape.25
  197.8 6.3 %all-to-all-start.2 = ((bf16[64,18,1024]{2,1,0:T(8,128)(2,1)}), bf16[64,18,1024]{2,1,0:T(8,128)(2,1)}, u32[]{:S(2)}, u32[]{:S(2)}) async-start(bf16[64,18,1024]{2,1,0:T(8,128)(2,1)} %reshape.25), calls=%async_computation.2 | async-start | bytes 6291456 | tf_op jit(solution)/shard_map/all_to_all | solution.py:64
  204.1 0.3 reduce-scatter.4.cloned.1.call-start
  204.3 1.6 pad_maximum_fusion
  205.9 2.6 copy.37
  208.5 69.0 %all-to-all-done.2 = bf16[64,18,1024]{2,1,0:T(8,128)(2,1)} async-done(((bf16[64,18,1024]{2,1,0:T(8,128)(2,1)}), bf16[64,18,1024]{2,1,0:T(8,128)(2,1)}, u32[]{:S(2)}, u32[]{:S(2)}) %all-to-all-start.2) | async-done | bytes 2359328 | tf_op jit(solution)/shard_map/all_to_all | solution.py:64
  277.5 5.3 %fusion.8 = bf16[128,1024]{1,0:T(8,128)(2,1)} fusion(bf16[64,18,1024]{2,1,0:T(8,128)(2,1)} %all-to-all-done.2, s32[64,128]{1,0:T(8,128)S(1)} %convolution_convert_fusion.4, pred[64,128]{1,0:T(8,128)(4,1)S(1)} %fusion.25), kind=kOutput, calls=%fused_computation.17 | convolution fusion | flops 302415872 | bytes 2662400 | tf_op jit(solution)/shard_map/ect,ecd->td/dot_general | solution.py:71
  282.8 1.2 copy.38
  284.0 0.7 slice_bitcast_fusion
  284.8 0.8 copy.36
  285.6 0.8 copy.35
  (15 shorter events, 0.7 us)
Async XLA Ops:
  7.2 2.0 copy-start
  13.0 85.1 %all-to-all-start = ((bf16[64,18,1024]{2,1,0:T(8,128)(2,1)}), bf16[64,18,1024]{2,1,0:T(8,128)(2,1)S(1)}, u32[]{:S(2)}, u32[]{:S(2)}) async-start(bf16[64,18,1024]{2,1,0:T(8,128)(2,1)} %copy.30), calls=%async_computation | async-start | bytes 6291456 | tf_op jit(solution)/shard_map/all_to_all | solution.py:57
  98.1 79.7 %all-to-all-start.1 = ((bf16[64,18,1024]{2,1,0:T(8,128)(2,1)}), bf16[64,18,1024]{2,1,0:T(8,128)(2,1)}, u32[]{:S(2)}, u32[]{:S(2)}) async-start(bf16[64,18,1024]{2,1,0:T(8,128)(2,1)} %copy.33), calls=%async_computation.1 | async-start | bytes 6291456 | tf_op jit(solution)/shard_map/all_to_all | solution.py:56
  104.4 77.8 %all-gather.2.cloned.1.call-start = ((), (), s32[]{:S(2)}) async-start(), calls=%async_computation.4 | async-start | bytes 2654208 | tf_op jit(solution)/shard_map/all_gather | solution.py:46
  182.1 4.5 %copy-start.1 = (bf16[1152,1024]{1,0:T(8,128)(2,1)S(1)}, bf16[1152,1024]{1,0:T(8,128)(2,1)}, u32[]{:S(2)}) copy-start(bf16[1152,1024]{1,0:T(8,128)(2,1)} %reshape.23) | copy-start | bytes 7077892
  186.6 1.7 copy-start.3
  188.3 1.7 copy-start.2
  197.8 79.7 %all-to-all-start.2 = ((bf16[64,18,1024]{2,1,0:T(8,128)(2,1)}), bf16[64,18,1024]{2,1,0:T(8,128)(2,1)}, u32[]{:S(2)}, u32[]{:S(2)}) async-start(bf16[64,18,1024]{2,1,0:T(8,128)(2,1)} %reshape.25), calls=%async_computation.2 | async-start | bytes 6291456 | tf_op jit(solution)/shard_map/all_to_all | solution.py:64
  204.1 78.8 %reduce-scatter.4.cloned.1.call-start = ((), (), s32[]{:S(2)}) async-start(), calls=%async_computation.5 | async-start | bytes 2654208
Sparse Core Ops, SparseCore 0:
  109.1 52.5 all-gather.1
  208.6 46.8 reduce-scatter.3

commit v3 on v2

v3 whole, which is shorter than its diff:
```python
import functools

import jax
import jax.numpy as jnp
from jax import lax
from jax.experimental import pallas as pl
from jax.experimental.pallas import tpu as pltpu
from jax.sharding import PartitionSpec as P

MESH = pl.DeviceIdType.MESH
F32 = jnp.float32
BF16 = jnp.bfloat16

NX, NY, NC, NZ = 4, 8, 2, 8
BLOCKS = 32
FULL = 16
CAP = 18
STEPS = ((4, 3), (3, 4))


def iota(shape, dim):
    return lax.broadcasted_iota(jnp.int32, shape, dim)


def y_shift(j, core):
    return j + 4 * (j // 3) + 4 * core * ((j // 2) % 2) * ((j + 1) % 2)


def far_first(k):
    return (2 + k) * (1 - k // 2) + (3 - k) * (k // 2)


def block_at(i):
    dx = far_first(i // 8)
    j = far_first((i // 2) % 4)
    return (dx * 4 + j) * 2 + i % 2


def dot_tn(a, b):
    return lax.dot_general(a, b, (((0,), (0,)), ((), ())), preferred_element_type=F32)


def dot_nt(a, b):
    return lax.dot_general(a, b, (((1,), (1,)), ((), ())), preferred_element_type=F32)


def kernel(
    tok,
    dout,
    comb,
    rout,
    gate,
    up,
    down,
    o_tok,
    o_gate,
    o_up,
    o_down,
    rank,
    scale,
    pick_lo,
    pick_hi,
    pick_left,
    w,
    sx,
    sg,
    rx,
    rg,
    xe,
    ge,
    dr,
    dph,
    sr,
    rr,
    wg,
    part,
    swap,
    swap_in,
    sem_xs,
    sem_xr,
    sem_gs,
    sem_gr,
    sem_rs,
    sem_rr,
    ag_s,
    ag_r,
    red_s,
    red_r,
    sw_s,
    sw_r,
):
    z = lax.axis_index("dp")
    e = lax.axis_index("expert")
    x, y, c = e // 16, (e // 2) % 8, e % 2
    b_own = y // 4
    b_oth = 1 - b_own
    n_tok, width = tok.shape
    hid = gate.shape[2]
    shard = width // NZ
    left = 2 * width
    quarter = width // 4
    rows_main = BLOCKS * FULL
    rows_all = BLOCKS * CAP
    partner = (z, x * 16 + ((y + 4) % 8) * 2 + c)

    def target(o):
        dx, j, dc = o // 8, (o // 2) % 4, o % 2
        return (x + dx) % 4, (y + y_shift(j, c)) % 8, (c + dc) % 2

    def forward(o):
        xd, yd, cd = target(o)
        return (z, xd * 16 + yd * 2 + cd)

    def backward(o):
        dx, j, dc = o // 8, (o // 2) % 4, o % 2
        cs = (c + dc) % 2
        return (z, ((x + 4 - dx) % 4) * 16 + ((y + 8 - y_shift(j, cs)) % 8) * 2 + cs)

    def z_next(d):
        return ((z + (1 if d == 0 else NZ - 1)) % NZ, e)

    barrier = pltpu.get_barrier_semaphore()

    @pl.loop(1, BLOCKS)
    def _(o):
        pl.semaphore_signal(barrier, inc=1, device_id=forward(o), device_id_type=MESH)
        pl.semaphore_signal(barrier, inc=1, device_id=backward(o), device_id_type=MESH)

    for d in range(2):
        pl.semaphore_signal(barrier, inc=1, device_id=z_next(d), device_id_type=MESH)
    pl.semaphore_signal(barrier, inc=1, device_id=partner, device_id_type=MESH)

    def slice_at(k):
        return pl.ds(pl.multiple_of(((z + k + 2 * NZ) % NZ) * shard, shard), shard)

    w[b_own, slice_at(0), :hid] = gate[0]
    w[b_own, slice_at(0), hid : 2 * hid] = up[0]
    w[b_own, slice_at(0), 2 * hid :] = down[0].T

    experts = NX * NY * NC
    ids = iota((experts, n_tok), 0)
    routes_t = rout[...].T
    comb_t = comb[...].T
    member = jnp.zeros((experts, n_tok), jnp.bool_)
    weight = jnp.zeros((experts, n_tok), F32)
    for k in range(rout.shape[1]):
        hit = routes_t[k : k + 1, :] == ids
        member = member | hit
        weight = weight + jnp.where(hit, comb_t[k : k + 1, :], 0.0)
    before = jnp.where(iota((n_tok, n_tok), 0) < iota((n_tok, n_tok), 1), 1.0, 0.0)
    count = jnp.dot(
        jnp.where(member, 1.0, 0.0).astype(BF16), before.astype(BF16), preferred_element_type=F32
    )
    rank[...] = jnp.where(member, count, -1.0)
    scale[...] = weight

    pl.semaphore_wait(barrier, 2 * (BLOCKS - 1) + 3)

    def swap_weights():
        return pltpu.make_async_remote_copy(
            src_ref=w.at[b_own, slice_at(0)],
            dst_ref=w.at[b_own, slice_at(0)],
            send_sem=sw_s.at[0],
            recv_sem=sw_r.at[0],
            device_id=partner,
            device_id_type=MESH,
        )

    def swap_weights_in():
        return pltpu.make_async_remote_copy(
            src_ref=w.at[b_oth, slice_at(0)],
            dst_ref=w.at[b_oth, slice_at(0)],
            send_sem=sw_s.at[0],
            recv_sem=sw_r.at[0],
            device_id=partner,
            device_id_type=MESH,
        )

    def gather_step(who, d, s, arriving=False):
        b = (b_own, b_oth)[who]
        sign = 1 if d == 0 else -1
        at = slice_at(-sign * (s + (1 if arriving else 0)))
        return pltpu.make_async_remote_copy(
            src_ref=w.at[b, at],
            dst_ref=w.at[b, at],
            send_sem=ag_s.at[who, d, s],
            recv_sem=ag_r.at[who, d, s],
            device_id=z_next(d),
            device_id_type=MESH,
        )

    swap_weights().start()
    for d in range(2):
        gather_step(0, d, 0).start()

    row = iota((3 * FULL, n_tok), 0)
    left_row = row % FULL
    is_hi = ((row // FULL) == 1) | (((row // FULL) == 2) & ((left_row % 4) >= 2))
    slot = jnp.where(row // FULL == 2, FULL + row % 2, row % FULL).astype(F32)
    q_row = iota((FULL, quarter), 0) // 4

    def pick_of(o):
        xd, yd, cd = target(o)
        lo = xd * 16 + (yd % 4) * 2 + cd
        chosen = jnp.where(is_hi, rank[pl.ds(lo + 8, 1), :], rank[pl.ds(lo, 1), :])
        return lo, chosen == slot

    def store_block(dst, o, block):
        dst[o, :, :width] = block[:FULL].astype(BF16)
        dst[o, :, width:left] = block[FULL : 2 * FULL].astype(BF16)
        rest = block[2 * FULL :]
        packed = jnp.zeros((FULL, quarter), F32)
        for q in range(4):
            packed = jnp.where(q_row == q, rest[:, q * quarter : (q + 1) * quarter], packed)
        dst[o, :, left:] = packed.astype(BF16)

    def send_block(src, dst, o, s_sem, r_sem, to):
        pltpu.make_async_remote_copy(
            src_ref=src.at[o],
            dst_ref=dst.at[o],
            send_sem=s_sem,
            recv_sem=r_sem,
            device_id=to,
            device_id_type=MESH,
        ).start()

    def whole(src, dst, s_sem, r_sem):
        return pltpu.make_async_remote_copy(
            src_ref=src.at[pl.ds(1, BLOCKS - 1)],
            dst_ref=dst.at[pl.ds(1, BLOCKS - 1)],
            send_sem=s_sem,
            recv_sem=r_sem,
            device_id=partner,
            device_id_type=MESH,
        )

    group = 4

    @pl.loop(0, BLOCKS // group)
    def _(i):
        picks = []
        for u in range(group):
            o = block_at(i * group + u)
            _, hit = pick_of(o)
            one_hot = jnp.where(hit, 1.0, 0.0).astype(BF16)
            pick_lo[o] = one_hot[:FULL]
            pick_hi[o] = one_hot[FULL : 2 * FULL]
            pick_left[o] = one_hot[2 * FULL :]
            picks.append(one_hot)
        block = jnp.dot(jnp.concatenate(picks, axis=0), tok[...], preferred_element_type=F32)
        for u in range(group):
            o = block_at(i * group + u)
            store_block(sx, o, block[u * 3 * FULL : (u + 1) * 3 * FULL])

            @pl.when(i * group + u < BLOCKS - 2)
            def _():
                send_block(sx, rx, o, sem_xs, sem_xr, forward(o))

    send_block(sx, rx, 1, sem_xs, sem_xr, forward(1))
    rx[0] = sx[0]
    swap_weights_in().wait_recv()
    for d in range(2):
        gather_step(1, d, 0).start()

    @pl.loop(0, BLOCKS // group)
    def _(i):
        picks, scales = [], []
        for u in range(group):
            o = block_at(i * group + u)
            lo, hit = pick_of(o)
            chosen = jnp.where(is_hi, scale[pl.ds(lo + 8, 1), :], scale[pl.ds(lo, 1), :])
            scales.append(jnp.sum(jnp.where(hit, chosen, 0.0), axis=1, keepdims=True))
            picks.append(jnp.where(hit, 1.0, 0.0).astype(BF16))
        block = jnp.dot(jnp.concatenate(picks, axis=0), dout[...], preferred_element_type=F32)
        block = block * jnp.concatenate(scales, axis=0)
        for u in range(group):
            o = block_at(i * group + u)
            store_block(sg, o, block[u * 3 * FULL : (u + 1) * 3 * FULL])

            @pl.when(i * group + u < BLOCKS - 2)
            def _():
                send_block(sg, rg, o, sem_gs, sem_gr, forward(o))

    send_block(sg, rg, 1, sem_gs, sem_gr, forward(1))
    rg[0] = sg[0]

    for s in range(1, 4):
        for who in range(2):
            for d in range(2):
                if s < STEPS[who][d]:
                    gather_step(who, d, s - 1, True).wait_recv()
                    gather_step(who, d, s).start()

    def unpack(src, dst):
        for b in range(2):
            dst[b, :rows_main, :] = src[:, :, b * width : (b + 1) * width].reshape(
                rows_main, width
            )
        rest = src[:, :, left:].reshape(rows_main, quarter)
        r = iota((4 * BLOCKS, rows_main), 0)
        base = ((r % (2 * BLOCKS)) // 2) * FULL + (r // (2 * BLOCKS)) * 2 + r % 2
        for q in range(4):
            take = jnp.where(iota((4 * BLOCKS, rows_main), 1) == base + 4 * q, 1.0, 0.0)
            part_q = jnp.dot(take.astype(BF16), rest, preferred_element_type=F32).astype(BF16)
            for b in range(2):
                dst[b, rows_main:, q * quarter : (q + 1) * quarter] = part_q[
                    b * 2 * BLOCKS : (b + 1) * 2 * BLOCKS
                ]

    whole(sx, rx, sem_xs, sem_xr).wait_recv()
    unpack(rx, xe)
    whole(sg, rg, sem_gs, sem_gr).wait_recv()
    unpack(rg, ge)
    for who in range(2):
        for d in range(2):
            gather_step(who, d, STEPS[who][d] - 1, True).wait_recv()

    chunk = 192

    def rows_of(b):
        @pl.loop(0, rows_all // chunk)
        def _(i):
            at = pl.ds(pl.multiple_of(i * chunk, chunk), chunk)
            pre = jnp.dot(xe[b, at, :], w[b, :, : 2 * hid], preferred_element_type=F32)
            d_hidden = jnp.dot(ge[b, at, :], w[b, :, 2 * hid :], preferred_element_type=F32)
            gate_pre, up_pre = pre[:, :hid], pre[:, hid:]
            sig = jax.nn.sigmoid(gate_pre)
            silu = gate_pre * sig
            d_gate = d_hidden * up_pre * sig * (1.0 + gate_pre * (1.0 - sig))
            dph[at, :hid] = d_gate.astype(BF16)
            dph[at, hid : 2 * hid] = (d_hidden * silu).astype(BF16)
            dph[at, 2 * hid :] = (silu * up_pre).astype(BF16)
            dr[b, at, :] = dot_nt(dph[at, : 2 * hid], w[b, :, : 2 * hid]).astype(BF16)

    def grads_of(b):
        for k in range(3):
            src = xe if k < 2 else ge
            total = dot_tn(dph[:, k * hid : (k + 1) * hid], src[b]).astype(BF16)
            for s in range(NZ):
                wg[b, s, k * hid : (k + 1) * hid, :] = total[:, s * shard : (s + 1) * shard]

    def red_step(who, d, s):
        b = (b_own, b_oth)[who]
        sign = 1 if d == 0 else -1
        k = STEPS[who][d] - s
        return pltpu.make_async_remote_copy(
            src_ref=wg.at[b, (z + sign * k + NZ) % NZ],
            dst_ref=part.at[who, d, s],
            send_sem=red_s.at[who, d, s],
            recv_sem=red_r.at[who, d, s],
            device_id=z_next(d),
            device_id_type=MESH,
        )

    rows_of(b_oth)
    grads_of(b_oth)
    for d in range(2):
        red_step(1, d, 0).start()
    rows_of(b_own)

    for b in range(2):
        sr[:, :, b * width : (b + 1) * width] = dr[b, :rows_main, :].reshape(BLOCKS, FULL, width)
    spread_row = iota((rows_main, 4 * BLOCKS), 0)
    spread = jnp.where(
        iota((rows_main, 4 * BLOCKS), 1)
        == ((spread_row // 2) % 2) * 2 * BLOCKS + (spread_row // FULL) * 2 + spread_row % 2,
        1.0,
        0.0,
    ).astype(BF16)
    tails = jnp.concatenate([dr[0, rows_main:, :], dr[1, rows_main:, :]], axis=0)
    tails = jnp.dot(spread, tails, preferred_element_type=F32)
    q_all = (iota((rows_main, quarter), 0) // 4) % 4
    packed = jnp.zeros((rows_main, quarter), F32)
    for q in range(4):
        packed = jnp.where(q_all == q, tails[:, q * quarter : (q + 1) * quarter], packed)
    sr[:, :, left:] = packed.astype(BF16).reshape(BLOCKS, FULL, quarter)

    @pl.loop(0, BLOCKS - 2)
    def _(i):
        o = block_at(i)
        send_block(sr, rr, o, sem_rs, sem_rr, backward(o))

    send_block(sr, rr, 1, sem_rs, sem_rr, backward(1))
    rr[0] = sr[0]

    grads_of(b_own)
    for d in range(2):
        red_step(0, d, 0).start()

    for s in range(1, 4):
        for who in (1, 0):
            for d in range(2):
                if s < STEPS[who][d]:
                    b = (b_own, b_oth)[who]
                    sign = 1 if d == 0 else -1
                    k = STEPS[who][d] - s
                    at = (z + sign * k + NZ) % NZ
                    red_step(who, d, s - 1).wait_recv()
                    wg[b, at] = (
                        wg[b, at].astype(F32) + part[who, d, s - 1].astype(F32)
                    ).astype(BF16)
                    red_step(who, d, s).start()

    def final(who):
        b = (b_own, b_oth)[who]
        total = wg[b, z].astype(F32)
        for d in range(2):
            last = STEPS[who][d] - 1
            red_step(who, d, last).wait_recv()
            total = total + part[who, d, last].astype(F32)
        return total

    swap[...] = final(1).astype(BF16)
    swap_grads = pltpu.make_async_remote_copy(
        src_ref=swap,
        dst_ref=swap_in,
        send_sem=sw_s.at[1],
        recv_sem=sw_r.at[1],
        device_id=partner,
        device_id_type=MESH,
    )
    swap_grads.start()

    whole(sr, rr, sem_rs, sem_rr).wait_recv()
    d_tok = dot_tn(
        pick_lo[...].reshape(rows_main, n_tok), rr[:, :, :width].reshape(rows_main, width)
    ) + dot_tn(
        pick_hi[...].reshape(rows_main, n_tok), rr[:, :, width:left].reshape(rows_main, width)
    )
    tail_pick = pick_left[...].reshape(rows_main, n_tok)
    tail = rr[:, :, left:].reshape(rows_main, quarter)
    q_pick = (iota((rows_main, n_tok), 0) // 4) % 4
    for q in range(4):
        one = jnp.where(q_pick == q, tail_pick.astype(F32), 0.0).astype(BF16)
        o_tok[:, q * quarter : (q + 1) * quarter] = (
            d_tok[:, q * quarter : (q + 1) * quarter] + dot_tn(one, tail)
        ).astype(BF16)

    total = final(0)
    swap_grads.wait_recv()
    total = total + swap_in[...].astype(F32)
    o_gate[0] = total[:hid].T
    o_up[0] = total[hid : 2 * hid].T
    o_down[0] = total[2 * hid :]

    whole(sx, rx, sem_xs, sem_xr).wait_send()
    whole(sg, rg, sem_gs, sem_gr).wait_send()
    whole(sr, rr, sem_rs, sem_rr).wait_send()
    swap_weights().wait_send()
    swap_grads.wait_send()
    for who in range(2):
        for d in range(2):
            for s in range(STEPS[who][d]):
                gather_step(who, d, s).wait_send()
                red_step(who, d, s).wait_send()


def body(tokens, d_output, combine, routes, gate_weight, up_weight, down_weight):
    n_tok, width = tokens.shape
    hid = gate_weight.shape[2]
    shard = width // NZ
    block = (BLOCKS, FULL, 2 * width + width // 4)
    rows = BLOCKS * CAP
    vmem = pl.BlockSpec(memory_space=pltpu.VMEM)
    dma = pltpu.SemaphoreType.DMA
    return pl.pallas_call(
        kernel,
        out_shape=(
            jax.ShapeDtypeStruct((n_tok, width), BF16),
            jax.ShapeDtypeStruct((1, shard, hid), F32),
            jax.ShapeDtypeStruct((1, shard, hid), F32),
            jax.ShapeDtypeStruct((1, hid, shard), F32),
        ),
        in_specs=[vmem] * 7,
        out_specs=(vmem,) * 4,
        scratch_shapes=[
            pltpu.VMEM((NX * NY * NC, n_tok), F32),
            pltpu.VMEM((NX * NY * NC, n_tok), F32),
            pltpu.VMEM((BLOCKS, FULL, n_tok), BF16),
            pltpu.VMEM((BLOCKS, FULL, n_tok), BF16),
            pltpu.VMEM((BLOCKS, FULL, n_tok), BF16),
            pltpu.VMEM((2, width, 3 * hid), BF16),
            pltpu.VMEM(block, BF16),
            pltpu.VMEM(block, BF16),
            pltpu.VMEM(block, BF16),
            pltpu.VMEM(block, BF16),
            pltpu.VMEM((2, rows, width), BF16),
            pltpu.VMEM((2, rows, width), BF16),
            pltpu.VMEM((2, rows, width), BF16),
            pltpu.VMEM((rows, 3 * hid), BF16),
            pltpu.VMEM(block, BF16),
            pltpu.VMEM(block, BF16),
            pltpu.VMEM((2, NZ, 3 * hid, shard), BF16),
            pltpu.VMEM((2, 2, 4, 3 * hid, shard), BF16),
            pltpu.VMEM((3 * hid, shard), BF16),
            pltpu.VMEM((3 * hid, shard), BF16),
            dma,
            dma,
            dma,
            dma,
            dma,
            dma,
            dma((2, 2, 4)),
            dma((2, 2, 4)),
            dma((2, 2, 4)),
            dma((2, 2, 4)),
            dma((2,)),
            dma((2,)),
        ],
        compiler_params=pltpu.CompilerParams(
            collective_id=0, has_side_effects=True, vmem_limit_bytes=56 << 20
        ),
        name="moe_backward",
    )(tokens, d_output, combine, routes, gate_weight, up_weight, down_weight)


def solution(mesh):
    placed = (
        P(("dp", "expert"), None),
        P(("dp", "expert"), None),
        P(("dp", "expert"), None),
        P(("dp", "expert"), None),
        P("expert", "dp", None),
        P("expert", "dp", None),
        P("expert", None, "dp"),
    )
    return jax.shard_map(
        body,
        mesh=mesh,
        in_specs=placed,
        out_specs=(
            P(("dp", "expert"), None),
            P("expert", "dp", None),
            P("expert", "dp", None),
            P("expert", None, "dp"),
        ),
        check_vma=False,
    )
```

time: 294 us -> 166 us (0.56)
  waiting for transfers between devices: 204 us -> 0 us
  Pallas kernels: 0 us -> 156 us
  starting transfers between devices: 24.6 us -> 0 us
  matrix products: 20.8 us -> 0 us
  local copies, waits for them, and re-layouts: 24.3 us -> 6.54 us
  between operations: 14.2 us -> 0.66 us
  other arithmetic: 5.18 us -> 0 us
    all_to_all x3 -> x0, waiting for transfers between devices: 204 us -> none  [the longest x1 69 us: body(): lax.all_to_all(d_rows.reshape(experts, capacity, model_width), 'expert',...]
    pallas_call x0 -> x1, Pallas kernels: none -> 156 us  [body(): pl.pallas_call(kernel, out_shape=(jax.ShapeDtypeStruct((n_tok, width), BF...]
    all_to_all x3 -> x0, starting transfers between devices: 24.1 us -> none  [the longest x1 11.6 us: body(): lax.all_to_all(send_grads, 'expert', split_axis=0, concat_axis=0, tiled=T...]
    dot_general x9 -> x0, matrix products: 20.8 us -> none  [the longest x1 5.34 us: body(): jnp.einsum('ect,ecd->td', pick, returned, preferred_element_type=jnp.floa...]
    reshape x3 -> x0, local copies, waits for them, and re-layouts: 9.05 us -> none  [the longest x1 4.32 us: body(): flat_inputs = recv_inputs.reshape(-1, model_width)]
    convert_element_type x2 -> x0, local copies, waits for them, and re-layouts: 6.09 us -> none  [the longest x1 3.06 us: body(): send_inputs = jnp.einsum('ect,td->ecd', pick, tokens, preferred_element_t...]
    concatenate x2 -> x0, other arithmetic: 3.29 us -> none  [the longest x1 1.68 us: body(): jnp.concatenate([gate_weight[0], up_weight[0], down_weight[0].T], axis=1)]
  transfers between devices with their start and end apart: 5 -> 0, of which waited for: 3 -> 0; matrix products, arithmetic and copies ran while one was open for 9% -> 0% of each run, Pallas kernels for 0% -> 0%
where the time goes in v3:
time: 166 us; the launch traced here: 163 us
  Pallas kernels  156 us (94%)
  local copies, waits for them, and re-layouts  6.54 us (4%)
    pallas_call x1, Pallas kernels, body(): pl.pallas_call(kernel, out_shape=(jax.ShapeDtypeStruct((n_tok, width), BF...  156 us
    unnamed x14, local copies, waits for them, and re-layouts  6.54 us

profile of v3, /device:TPU:1, one launch (start us, length us, event | category | flops | bytes accessed | tf_op | source)
XLA Modules:
  0.0 163.0 jit_solution(17930488821377385501)
XLA Ops:
  0.6 0.0 copy-start.3
  0.6 1.4 copy.11.comb
  2.1 0.0 copy-done.3
  2.1 0.7 copy.12.rout
  2.8 155.8 %moe_backward.1 = (bf16[128,1024]{1,0:T(8,128)(2,1)}, f32[1,128,384]{2,1,0:T(8,128)}, f32[1,128,384]{2,1,0:T(8,128)}, f32[1,384,128]{2,1,0:T(8,128)}) custom-call(bf16[128,1024]{1,0:T(8,128)(2,1)} %tok.1, bf16[128,1024]{1,0:T(8,128)(2,1)} %dout.1, f32[128,8]{1,0:T(8,128)} %copy.11.comb, s32[128,8]{1,0:T(8,128)} %copy.12.rout, bf16[1,128,384]{2,1,0:T(8,128)(2,1)} %gate.1, ...), custom_call_target="tpu_custom_call" | custom-call | tf_op jit(solution)/shard_map/moe_backward/pallas_call | solution.py:466
  158.6 0.0 copy-start.2
  158.6 1.7 %copy.17 = bf16[128,1024]{1,0:T(8,128)(2,1)} copy(bf16[128,1024]{1,0:T(8,128)(2,1)} %get-tuple-element.8) | data formatting | bytes 524288
  160.3 0.0 copy-done.2
  160.3 0.0 copy-start.1
  160.3 0.7 copy.18
  161.0 0.3 copy-done.1
  161.3 0.0 copy-start
  161.3 0.7 copy.19
  162.0 0.3 copy-done
  162.3 0.7 copy.20
Async XLA Ops:
  0.6 1.4 copy-start.3
  158.6 1.7 %copy-start.2 = (f32[1,128,384]{2,1,0:T(8,128)S(1)}, f32[1,128,384]{2,1,0:T(8,128)}, u32[]{:S(2)}) copy-start(f32[1,128,384]{2,1,0:T(8,128)} %get-tuple-element.9) | copy-start | bytes 589828
  160.3 1.0 copy-start.1
  161.3 1.0 copy-start

commit v4 on v3

--- a/solution.py
+++ b/solution.py
@@ -15,6 +15,7 @@
 BLOCKS = 32
 FULL = 16
 CAP = 18
+SELF = 3
 STEPS = ((4, 3), (3, 4))
 
 
@@ -31,9 +32,9 @@
 
 
 def block_at(i):
-    dx = far_first(i // 8)
-    j = far_first((i // 2) % 4)
-    return (dx * 4 + j) * 2 + i % 2
+    dx = far_first(i % 4)
+    j = (dx + 4 - (i // 4) % 4) % 4
+    return (dx * 4 + j) * 2 + i // 16
 
 
 def dot_tn(a, b):
@@ -69,6 +70,7 @@
     xe,
     ge,
     dr,
+    pre,
     dph,
     sr,
     rr,
@@ -139,11 +141,10 @@
 
     experts = NX * NY * NC
     ids = iota((experts, n_tok), 0)
-    routes_t = rout[...].T
-    comb_t = comb[...].T
+    routes_t, comb_t = rout[...], comb[...]
     member = jnp.zeros((experts, n_tok), jnp.bool_)
     weight = jnp.zeros((experts, n_tok), F32)
-    for k in range(rout.shape[1]):
+    for k in range(rout.shape[0]):
         hit = routes_t[k : k + 1, :] == ids
         member = member | hit
         weight = weight + jnp.where(hit, comb_t[k : k + 1, :], 0.0)
@@ -188,6 +189,12 @@
             device_id=z_next(d),
             device_id_type=MESH,
         )
+
+    def gather_next(who, s):
+        for d in range(2):
+            if s < STEPS[who][d]:
+                gather_step(who, d, s - 1, True).wait_recv()
+                gather_step(who, d, s).start()
 
     swap_weights().start()
     for d in range(2):
@@ -252,15 +259,12 @@
             o = block_at(i * group + u)
             store_block(sx, o, block[u * 3 * FULL : (u + 1) * 3 * FULL])
 
-            @pl.when(i * group + u < BLOCKS - 2)
+            @pl.when(i * group + u != SELF)
             def _():
                 send_block(sx, rx, o, sem_xs, sem_xr, forward(o))
 
-    send_block(sx, rx, 1, sem_xs, sem_xr, forward(1))
     rx[0] = sx[0]
-    swap_weights_in().wait_recv()
-    for d in range(2):
-        gather_step(1, d, 0).start()
+    gather_next(0, 1)
 
     @pl.loop(0, BLOCKS // group)
     def _(i):
@@ -277,19 +281,19 @@
             o = block_at(i * group + u)
             store_block(sg, o, block[u * 3 * FULL : (u + 1) * 3 * FULL])
 
-            @pl.when(i * group + u < BLOCKS - 2)
+            @pl.when(i * group + u != SELF)
             def _():
                 send_block(sg, rg, o, sem_gs, sem_gr, forward(o))
 
-    send_block(sg, rg, 1, sem_gs, sem_gr, forward(1))
     rg[0] = sg[0]
 
+    gather_next(0, 2)
+    swap_weights_in().wait_recv()
+    for d in range(2):
+        gather_step(1, d, 0).start()
+    gather_next(0, 3)
     for s in range(1, 4):
-        for who in range(2):
-            for d in range(2):
-                if s < STEPS[who][d]:
-                    gather_step(who, d, s - 1, True).wait_recv()
-                    gather_step(who, d, s).start()
+        gather_next(1, s)
 
     def unpack(src, dst):
         for b in range(2):
@@ -309,33 +313,44 @@
 
     whole(sx, rx, sem_xs, sem_xr).wait_recv()
     unpack(rx, xe)
-    whole(sg, rg, sem_gs, sem_gr).wait_recv()
-    unpack(rg, ge)
     for who in range(2):
         for d in range(2):
             gather_step(who, d, STEPS[who][d] - 1, True).wait_recv()
 
     chunk = 192
 
-    def rows_of(b):
+    def chunk_at(i):
+        return pl.ds(pl.multiple_of(i * chunk, chunk), chunk)
+
+    def forward_rows(b):
         @pl.loop(0, rows_all // chunk)
         def _(i):
-            at = pl.ds(pl.multiple_of(i * chunk, chunk), chunk)
-            pre = jnp.dot(xe[b, at, :], w[b, :, : 2 * hid], preferred_element_type=F32)
+            at = chunk_at(i)
+            pre[b, at, :] = jnp.dot(xe[b, at, :], w[b, :, : 2 * hid], preferred_element_type=F32)
+
+    def backward_rows(b):
+        @pl.loop(0, rows_all // chunk)
+        def _(i):
+            at = chunk_at(i)
             d_hidden = jnp.dot(ge[b, at, :], w[b, :, 2 * hid :], preferred_element_type=F32)
-            gate_pre, up_pre = pre[:, :hid], pre[:, hid:]
+            gate_pre, up_pre = pre[b, at, :hid], pre[b, at, hid:]
             sig = jax.nn.sigmoid(gate_pre)
             silu = gate_pre * sig
             d_gate = d_hidden * up_pre * sig * (1.0 + gate_pre * (1.0 - sig))
-            dph[at, :hid] = d_gate.astype(BF16)
-            dph[at, hid : 2 * hid] = (d_hidden * silu).astype(BF16)
-            dph[at, 2 * hid :] = (silu * up_pre).astype(BF16)
-            dr[b, at, :] = dot_nt(dph[at, : 2 * hid], w[b, :, : 2 * hid]).astype(BF16)
+            dph[b, at, :hid] = d_gate.astype(BF16)
+            dph[b, at, hid : 2 * hid] = (d_hidden * silu).astype(BF16)
+            dph[b, at, 2 * hid :] = (silu * up_pre).astype(BF16)
+
+    def input_rows(b):
+        @pl.loop(0, rows_all // chunk)
+        def _(i):
+            at = chunk_at(i)
+            dr[b, at, :] = dot_nt(dph[b, at, : 2 * hid], w[b, :, : 2 * hid]).astype(BF16)
 
     def grads_of(b):
         for k in range(3):
             src = xe if k < 2 else ge
-            total = dot_tn(dph[:, k * hid : (k + 1) * hid], src[b]).astype(BF16)
+            total = dot_tn(dph[b, :, k * hid : (k + 1) * hid], src[b]).astype(BF16)
             for s in range(NZ):
                 wg[b, s, k * hid : (k + 1) * hid, :] = total[:, s * shard : (s + 1) * shard]
 
@@ -352,11 +367,37 @@
             device_id_type=MESH,
         )
 
-    rows_of(b_oth)
-    grads_of(b_oth)
-    for d in range(2):
-        red_step(1, d, 0).start()
-    rows_of(b_own)
+    def red_next(who, s):
+        b = (b_own, b_oth)[who]
+        for d in range(2):
+            if s < STEPS[who][d]:
+                sign = 1 if d == 0 else -1
+                at = (z + sign * (STEPS[who][d] - s) + NZ) % NZ
+                red_step(who, d, s - 1).wait_recv()
+                wg[b, at] = (
+                    wg[b, at].astype(F32) + part[who, d, s - 1].astype(F32)
+                ).astype(BF16)
+                red_step(who, d, s).start()
+
+    @pl.loop(0, 2)
+    def _(b):
+        forward_rows(b)
+
+    whole(sg, rg, sem_gs, sem_gr).wait_recv()
+    unpack(rg, ge)
+
+    for who in (1, 0):
+        b = (b_own, b_oth)[who]
+        backward_rows(b)
+        grads_of(b)
+        if who == 0:
+            red_next(1, 1)
+        for d in range(2):
+            red_step(who, d, 0).start()
+
+    @pl.loop(0, 2)
+    def _(b):
+        input_rows(b)
 
     for b in range(2):
         sr[:, :, b * width : (b + 1) * width] = dr[b, :rows_main, :].reshape(BLOCKS, FULL, width)
@@ -375,31 +416,17 @@
         packed = jnp.where(q_all == q, tails[:, q * quarter : (q + 1) * quarter], packed)
     sr[:, :, left:] = packed.astype(BF16).reshape(BLOCKS, FULL, quarter)
 
-    @pl.loop(0, BLOCKS - 2)
+    @pl.loop(0, BLOCKS - 1)
     def _(i):
-        o = block_at(i)
+        o = block_at((i + SELF + 1) % BLOCKS)
         send_block(sr, rr, o, sem_rs, sem_rr, backward(o))
 
-    send_block(sr, rr, 1, sem_rs, sem_rr, backward(1))
     rr[0] = sr[0]
 
-    grads_of(b_own)
-    for d in range(2):
-        red_step(0, d, 0).start()
-
-    for s in range(1, 4):
-        for who in (1, 0):
-            for d in range(2):
-                if s < STEPS[who][d]:
-                    b = (b_own, b_oth)[who]
-                    sign = 1 if d == 0 else -1
-                    k = STEPS[who][d] - s
-                    at = (z + sign * k + NZ) % NZ
-                    red_step(who, d, s - 1).wait_recv()
-                    wg[b, at] = (
-                        wg[b, at].astype(F32) + part[who, d, s - 1].astype(F32)
-                    ).astype(BF16)
-                    red_step(who, d, s).start()
+    red_next(1, 2)
+    red_next(0, 1)
+    red_next(1, 3)
+    red_next(0, 2)
 
     def final(who):
         b = (b_own, b_oth)[who]
@@ -420,6 +447,7 @@
         device_id_type=MESH,
     )
     swap_grads.start()
+    red_next(0, 3)
 
     whole(sr, rr, sem_rs, sem_rr).wait_recv()
     d_tok = dot_tn(
@@ -487,7 +515,8 @@
             pltpu.VMEM((2, rows, width), BF16),
             pltpu.VMEM((2, rows, width), BF16),
             pltpu.VMEM((2, rows, width), BF16),
-            pltpu.VMEM((rows, 3 * hid), BF16),
+            pltpu.VMEM((2, rows, 2 * hid), F32),
+            pltpu.VMEM((2, rows, 3 * hid), BF16),
             pltpu.VMEM(block, BF16),
             pltpu.VMEM(block, BF16),
             pltpu.VMEM((2, NZ, 3 * hid, shard), BF16),
@@ -511,7 +540,7 @@
             collective_id=0, has_side_effects=True, vmem_limit_bytes=56 << 20
         ),
         name="moe_backward",
-    )(tokens, d_output, combine, routes, gate_weight, up_weight, down_weight)
+    )(tokens, d_output, combine.T, routes.T, gate_weight, up_weight, down_weight)
 
 
 def solution(mesh):

time: 166 us -> 150 us (0.904)
  the two profiles are of different devices: /device:TPU:1 before, /device:TPU:48 now
where the time goes in v4:
time: 150 us
  Pallas kernels  145 us (97%)
  local copies, waits for them, and re-layouts  4.38 us (3%)
    pallas_call x1, Pallas kernels, body(): pl.pallas_call(kernel, out_shape=(jax.ShapeDtypeStruct((n_tok, width), BF...  145 us
    unnamed x10, local copies, waits for them, and re-layouts  4.38 us

profile of v4, /device:TPU:48, one launch (start us, length us, event | category | flops | bytes accessed | tf_op | source)
XLA Modules:
  0.0 149.7 jit_solution(1252357434337339974)
XLA Ops:
  0.6 144.7 %moe_backward.1 = (bf16[128,1024]{1,0:T(8,128)(2,1)}, f32[1,128,384]{2,1,0:T(8,128)}, f32[1,128,384]{2,1,0:T(8,128)}, f32[1,384,128]{2,1,0:T(8,128)}) custom-call(bf16[128,1024]{1,0:T(8,128)(2,1)} %tok.1, bf16[128,1024]{1,0:T(8,128)(2,1)} %dout.1, f32[8,128]{1,0:T(8,128)} %bitcast.2, s32[8,128]{1,0:T(8,128)} %bitcast.3, bf16[1,128,384]{2,1,0:T(8,128)(2,1)} %gate.1, ...), custom_call_target="tpu_custom_call" | custom-call | tf_op jit(solution)/shard_map/moe_backward/pallas_call | solution.py:494
  145.3 0.0 copy-start.2
  145.3 1.7 %copy.15 = bf16[128,1024]{1,0:T(8,128)(2,1)} copy(bf16[128,1024]{1,0:T(8,128)(2,1)} %get-tuple-element.8) | data formatting | bytes 524288
  147.1 0.0 copy-done.2
  147.1 0.0 copy-start.1
  147.1 0.7 copy.16
  147.7 0.3 copy-done.1
  148.1 0.0 copy-start
  148.1 0.7 copy.17
  148.7 0.3 copy-done
  149.1 0.7 copy.18
Async XLA Ops:
  145.3 1.7 %copy-start.2 = (f32[1,128,384]{2,1,0:T(8,128)S(1)}, f32[1,128,384]{2,1,0:T(8,128)}, u32[]{:S(2)}) copy-start(f32[1,128,384]{2,1,0:T(8,128)} %get-tuple-element.9) | copy-start | bytes 589828
  147.1 1.0 copy-start.1
  148.1 1.0 copy-start

commit v5 on v4

--- a/solution.py
+++ b/solution.py
@@ -16,7 +16,10 @@
 FULL = 16
 CAP = 18
 SELF = 3
-STEPS = ((4, 3), (3, 4))
+NEAR = 4
+Y_ORDER = (1, 3, 2)
+X_ORDER = (2, 1, 3, 0)
+STEPS = 4
 
 
 def iota(shape, dim):
@@ -34,7 +37,7 @@
 def block_at(i):
     dx = far_first(i % 4)
     j = (dx + 4 - (i // 4) % 4) % 4
-    return (dx * 4 + j) * 2 + i // 16
+    return (dx * 2 + i // 16) * 4 + j
 
 
 def dot_tn(a, b):
@@ -59,6 +62,10 @@
     o_down,
     rank,
     scale,
+    yr,
+    yc,
+    yx,
+    yg,
     pick_lo,
     pick_hi,
     pick_left,
@@ -84,6 +91,8 @@
     sem_gr,
     sem_rs,
     sem_rr,
+    sem_ys,
+    sem_yr,
     ag_s,
     ag_r,
     red_s,
@@ -106,7 +115,7 @@
     partner = (z, x * 16 + ((y + 4) % 8) * 2 + c)
 
     def target(o):
-        dx, j, dc = o // 8, (o // 2) % 4, o % 2
+        dx, j, dc = o // 8, o % 4, (o // 4) % 2
         return (x + dx) % 4, (y + y_shift(j, c)) % 8, (c + dc) % 2
 
     def forward(o):
@@ -114,7 +123,7 @@
         return (z, xd * 16 + yd * 2 + cd)
 
     def backward(o):
-        dx, j, dc = o // 8, (o // 2) % 4, o % 2
+        dx, j, dc = o // 8, o % 4, (o // 4) % 2
         cs = (c + dc) % 2
         return (z, ((x + 4 - dx) % 4) * 16 + ((y + 8 - y_shift(j, cs)) % 8) * 2 + cs)
 
@@ -140,20 +149,27 @@
     w[b_own, slice_at(0), 2 * hid :] = down[0].T
 
     experts = NX * NY * NC
-    ids = iota((experts, n_tok), 0)
-    routes_t, comb_t = rout[...], comb[...]
-    member = jnp.zeros((experts, n_tok), jnp.bool_)
-    weight = jnp.zeros((experts, n_tok), F32)
-    for k in range(rout.shape[0]):
-        hit = routes_t[k : k + 1, :] == ids
-        member = member | hit
-        weight = weight + jnp.where(hit, comb_t[k : k + 1, :], 0.0)
-    before = jnp.where(iota((n_tok, n_tok), 0) < iota((n_tok, n_tok), 1), 1.0, 0.0)
-    count = jnp.dot(
-        jnp.where(member, 1.0, 0.0).astype(BF16), before.astype(BF16), preferred_element_type=F32
-    )
-    rank[...] = jnp.where(member, count, -1.0)
-    scale[...] = weight
+    before = jnp.where(iota((n_tok, n_tok), 0) < iota((n_tok, n_tok), 1), 1.0, 0.0).astype(BF16)
+
+    def slots_of(j):
+        ids = iota((experts, n_tok), 0)
+        member = jnp.zeros((experts, n_tok), jnp.bool_)
+        weight = jnp.zeros((experts, n_tok), F32)
+        for k in range(rout.shape[0]):
+            hit = yr[j, k : k + 1, :] == ids
+            member = member | hit
+            weight = weight + jnp.where(hit, yc[j, k : k + 1, :], 0.0)
+        count = jnp.dot(
+            jnp.where(member, 1.0, 0.0).astype(BF16), before, preferred_element_type=F32
+        )
+        rank[j] = jnp.where(member, count, -1.0)
+        scale[j] = weight
+
+    yr[0] = rout[...]
+    yc[0] = comb[...]
+    yx[0] = tok[...]
+    yg[0] = dout[...]
+    slots_of(0)
 
     pl.semaphore_wait(barrier, 2 * (BLOCKS - 1) + 3)
 
@@ -181,6 +197,10 @@
         b = (b_own, b_oth)[who]
         sign = 1 if d == 0 else -1
         at = slice_at(-sign * (s + (1 if arriving else 0)))
+        if s == STEPS - 1:
+            half = shard // 2
+            start = ((z - sign * (s + (1 if arriving else 0)) + 2 * NZ) % NZ) * shard
+            at = pl.ds(pl.multiple_of(start + d * half, half), half)
         return pltpu.make_async_remote_copy(
             src_ref=w.at[b, at],
             dst_ref=w.at[b, at],
@@ -192,13 +212,32 @@
 
     def gather_next(who, s):
         for d in range(2):
-            if s < STEPS[who][d]:
+            if s < STEPS:
                 gather_step(who, d, s - 1, True).wait_recv()
                 gather_step(who, d, s).start()
+
+    def y_copy(j, a):
+        return pltpu.make_async_remote_copy(
+            src_ref=(rout, comb, tok, dout)[a],
+            dst_ref=(yr, yc, yx, yg)[a].at[j],
+            send_sem=sem_ys.at[j, a],
+            recv_sem=sem_yr.at[j, a],
+            device_id=(z, x * 16 + ((y + y_shift(j, c)) % 8) * 2 + c),
+            device_id_type=MESH,
+        )
 
     swap_weights().start()
     for d in range(2):
         gather_step(0, d, 0).start()
+    for a in range(2):
+        for j in Y_ORDER:
+            y_copy(j, a).start()
+    for j in Y_ORDER[:2]:
+        y_copy(j, 2).start()
+    for j in Y_ORDER[:2]:
+        y_copy(j, 3).start()
+    for a in (2, 3):
+        y_copy(Y_ORDER[2], a).start()
 
     row = iota((3 * FULL, n_tok), 0)
     left_row = row % FULL
@@ -206,11 +245,9 @@
     slot = jnp.where(row // FULL == 2, FULL + row % 2, row % FULL).astype(F32)
     q_row = iota((FULL, quarter), 0) // 4
 
-    def pick_of(o):
-        xd, yd, cd = target(o)
-        lo = xd * 16 + (yd % 4) * 2 + cd
-        chosen = jnp.where(is_hi, rank[pl.ds(lo + 8, 1), :], rank[pl.ds(lo, 1), :])
-        return lo, chosen == slot
+    def pick_of(j, lo):
+        chosen = jnp.where(is_hi, rank[j, pl.ds(lo + 8, 1), :], rank[j, pl.ds(lo, 1), :])
+        return chosen == slot
 
     def store_block(dst, o, block):
         dst[o, :, :width] = block[:FULL].astype(BF16)
@@ -231,69 +268,88 @@
             device_id_type=MESH,
         ).start()
 
-    def whole(src, dst, s_sem, r_sem):
+    def whole(src, dst, s_sem, r_sem, first):
         return pltpu.make_async_remote_copy(
-            src_ref=src.at[pl.ds(1, BLOCKS - 1)],
-            dst_ref=dst.at[pl.ds(1, BLOCKS - 1)],
+            src_ref=src.at[pl.ds(first, BLOCKS - first)],
+            dst_ref=dst.at[pl.ds(first, BLOCKS - first)],
             send_sem=s_sem,
             recv_sem=r_sem,
             device_id=partner,
             device_id_type=MESH,
         )
 
-    group = 4
-
-    @pl.loop(0, BLOCKS // group)
-    def _(i):
-        picks = []
-        for u in range(group):
-            o = block_at(i * group + u)
-            _, hit = pick_of(o)
-            one_hot = jnp.where(hit, 1.0, 0.0).astype(BF16)
+    def dispatch(j, scaled):
+        rows_in, out, land = (yg, sg, rg) if scaled else (yx, sx, rx)
+        s_sem, r_sem = (sem_gs, sem_gr) if scaled else (sem_xs, sem_xr)
+
+        @pl.loop(0, 2)
+        def _(dc):
+            picks, scales = [], []
+            for dx in X_ORDER:
+                lo = ((x + dx) % 4) * 16 + (y % 4) * 2 + (c + dc) % 2
+                hit = pick_of(j, lo)
+                if scaled:
+                    chosen = jnp.where(
+                        is_hi, scale[j, pl.ds(lo + 8, 1), :], scale[j, pl.ds(lo, 1), :]
+                    )
+                    scales.append(jnp.sum(jnp.where(hit, chosen, 0.0), axis=1, keepdims=True))
+                picks.append(jnp.where(hit, 1.0, 0.0).astype(BF16))
+            block = jnp.dot(
+                jnp.concatenate(picks, axis=0), rows_in[j], preferred_element_type=F32
+            )
+            if scaled:
+                block = block * jnp.concatenate(scales, axis=0)
+            for u, dx in enumerate(X_ORDER):
+                o = (dx * 2 + dc) * 4 + j
+                store_block(out, o, block[u * 3 * FULL : (u + 1) * 3 * FULL])
+                to = (z, ((x + dx) % 4) * 16 + y * 2 + (c + dc) % 2)
+                if dx:
+                    send_block(out, land, o, s_sem, r_sem, to)
+                else:
+
+                    @pl.when(dc == 1)
+                    def _():
+                        send_block(out, land, o, s_sem, r_sem, to)
+
+        land[j] = out[j]
+
+    def own_picks():
+        @pl.loop(0, BLOCKS)
+        def _(o):
+            xd, yd, cd = target(o)
+            one_hot = jnp.where(
+                pick_of(0, xd * 16 + (yd % 4) * 2 + cd), 1.0, 0.0
+            ).astype(BF16)
             pick_lo[o] = one_hot[:FULL]
             pick_hi[o] = one_hot[FULL : 2 * FULL]
             pick_left[o] = one_hot[2 * FULL :]
-            picks.append(one_hot)
-        block = jnp.dot(jnp.concatenate(picks, axis=0), tok[...], preferred_element_type=F32)
-        for u in range(group):
-            o = block_at(i * group + u)
-            store_block(sx, o, block[u * 3 * FULL : (u + 1) * 3 * FULL])
-
-            @pl.when(i * group + u != SELF)
-            def _():
-                send_block(sx, rx, o, sem_xs, sem_xr, forward(o))
-
-    rx[0] = sx[0]
+
+    def rows_from(j, scaled):
+        y_copy(j, 2 + scaled).wait_recv()
+        dispatch(j, bool(scaled))
+
+    dispatch(0, False)
+    dispatch(0, True)
+    for j in Y_ORDER:
+        for a in range(2):
+            y_copy(j, a).wait_recv()
+        slots_of(j)
     gather_next(0, 1)
-
-    @pl.loop(0, BLOCKS // group)
-    def _(i):
-        picks, scales = [], []
-        for u in range(group):
-            o = block_at(i * group + u)
-            lo, hit = pick_of(o)
-            chosen = jnp.where(is_hi, scale[pl.ds(lo + 8, 1), :], scale[pl.ds(lo, 1), :])
-            scales.append(jnp.sum(jnp.where(hit, chosen, 0.0), axis=1, keepdims=True))
-            picks.append(jnp.where(hit, 1.0, 0.0).astype(BF16))
-        block = jnp.dot(jnp.concatenate(picks, axis=0), dout[...], preferred_element_type=F32)
-        block = block * jnp.concatenate(scales, axis=0)
-        for u in range(group):
-            o = block_at(i * group + u)
-            store_block(sg, o, block[u * 3 * FULL : (u + 1) * 3 * FULL])
-
-            @pl.when(i * group + u != SELF)
-            def _():
-                send_block(sg, rg, o, sem_gs, sem_gr, forward(o))
-
-    rg[0] = sg[0]
-
-    gather_next(0, 2)
+    rows_from(Y_ORDER[0], 0)
+    rows_from(Y_ORDER[1], 0)
     swap_weights_in().wait_recv()
     for d in range(2):
         gather_step(1, d, 0).start()
+    gather_next(0, 2)
+    rows_from(Y_ORDER[0], 1)
+    rows_from(Y_ORDER[1], 1)
+    gather_next(1, 1)
     gather_next(0, 3)
-    for s in range(1, 4):
-        gather_next(1, s)
+    rows_from(Y_ORDER[2], 0)
+    rows_from(Y_ORDER[2], 1)
+    gather_next(1, 2)
+    own_picks()
+    gather_next(1, 3)
 
     def unpack(src, dst):
         for b in range(2):
@@ -311,11 +367,11 @@
                     b * 2 * BLOCKS : (b + 1) * 2 * BLOCKS
                 ]
 
-    whole(sx, rx, sem_xs, sem_xr).wait_recv()
+    whole(sx, rx, sem_xs, sem_xr, NEAR).wait_recv()
     unpack(rx, xe)
     for who in range(2):
         for d in range(2):
-            gather_step(who, d, STEPS[who][d] - 1, True).wait_recv()
+            gather_step(who, d, STEPS - 1, True).wait_recv()
 
     chunk = 192
 
@@ -354,13 +410,16 @@
             for s in range(NZ):
                 wg[b, s, k * hid : (k + 1) * hid, :] = total[:, s * shard : (s + 1) * shard]
 
+    half_rows = 3 * hid // 2
+
     def red_step(who, d, s):
         b = (b_own, b_oth)[who]
         sign = 1 if d == 0 else -1
-        k = STEPS[who][d] - s
+        k = STEPS - s
+        span = pl.ds(d * half_rows, half_rows) if s == 0 else pl.ds(0, 2 * half_rows)
         return pltpu.make_async_remote_copy(
-            src_ref=wg.at[b, (z + sign * k + NZ) % NZ],
-            dst_ref=part.at[who, d, s],
+            src_ref=wg.at[b, (z + sign * k + NZ) % NZ, span],
+            dst_ref=part.at[who, d, s, span],
             send_sem=red_s.at[who, d, s],
             recv_sem=red_r.at[who, d, s],
             device_id=z_next(d),
@@ -370,12 +429,13 @@
     def red_next(who, s):
         b = (b_own, b_oth)[who]
         for d in range(2):
-            if s < STEPS[who][d]:
+            if s < STEPS:
                 sign = 1 if d == 0 else -1
-                at = (z + sign * (STEPS[who][d] - s) + NZ) % NZ
+                at = (z + sign * (STEPS - s) + NZ) % NZ
                 red_step(who, d, s - 1).wait_recv()
-                wg[b, at] = (
-                    wg[b, at].astype(F32) + part[who, d, s - 1].astype(F32)
+                span = pl.ds(d * half_rows, half_rows) if s == 1 else pl.ds(0, 2 * half_rows)
+                wg[b, at, span, :] = (
+                    wg[b, at, span, :].astype(F32) + part[who, d, s - 1, span, :].astype(F32)
                 ).astype(BF16)
                 red_step(who, d, s).start()
 
@@ -383,7 +443,7 @@
     def _(b):
         forward_rows(b)
 
-    whole(sg, rg, sem_gs, sem_gr).wait_recv()
+    whole(sg, rg, sem_gs, sem_gr, NEAR).wait_recv()
     unpack(rg, ge)
 
     for who in (1, 0):
@@ -432,7 +492,7 @@
         b = (b_own, b_oth)[who]
         total = wg[b, z].astype(F32)
         for d in range(2):
-            last = STEPS[who][d] - 1
+            last = STEPS - 1
             red_step(who, d, last).wait_recv()
             total = total + part[who, d, last].astype(F32)
         return total
@@ -449,7 +509,7 @@
     swap_grads.start()
     red_next(0, 3)
 
-    whole(sr, rr, sem_rs, sem_rr).wait_recv()
+    whole(sr, rr, sem_rs, sem_rr, 1).wait_recv()
     d_tok = dot_tn(
         pick_lo[...].reshape(rows_main, n_tok), rr[:, :, :width].reshape(rows_main, width)
     ) + dot_tn(
@@ -471,14 +531,17 @@
     o_up[0] = total[hid : 2 * hid].T
     o_down[0] = total[2 * hid :]
 
-    whole(sx, rx, sem_xs, sem_xr).wait_send()
-    whole(sg, rg, sem_gs, sem_gr).wait_send()
-    whole(sr, rr, sem_rs, sem_rr).wait_send()
+    whole(sx, rx, sem_xs, sem_xr, NEAR).wait_send()
+    whole(sg, rg, sem_gs, sem_gr, NEAR).wait_send()
+    whole(sr, rr, sem_rs, sem_rr, 1).wait_send()
     swap_weights().wait_send()
+    for j in Y_ORDER:
+        for a in range(4):
+            y_copy(j, a).wait_send()
     swap_grads.wait_send()
     for who in range(2):
         for d in range(2):
-            for s in range(STEPS[who][d]):
+            for s in range(STEPS):
                 gather_step(who, d, s).wait_send()
                 red_step(who, d, s).wait_send()
 
@@ -486,6 +549,7 @@
 def body(tokens, d_output, combine, routes, gate_weight, up_weight, down_weight):
     n_tok, width = tokens.shape
     hid = gate_weight.shape[2]
+    top = routes.shape[1]
     shard = width // NZ
     block = (BLOCKS, FULL, 2 * width + width // 4)
     rows = BLOCKS * CAP
@@ -502,8 +566,12 @@
         in_specs=[vmem] * 7,
         out_specs=(vmem,) * 4,
         scratch_shapes=[
-            pltpu.VMEM((NX * NY * NC, n_tok), F32),
-            pltpu.VMEM((NX * NY * NC, n_tok), F32),
+            pltpu.VMEM((4, NX * NY * NC, n_tok), F32),
+            pltpu.VMEM((4, NX * NY * NC, n_tok), F32),
+            pltpu.VMEM((4, top, n_tok), jnp.int32),
+            pltpu.VMEM((4, top, n_tok), F32),
+            pltpu.VMEM((4, n_tok, width), BF16),
+            pltpu.VMEM((4, n_tok, width), BF16),
             pltpu.VMEM((BLOCKS, FULL, n_tok), BF16),
             pltpu.VMEM((BLOCKS, FULL, n_tok), BF16),
             pltpu.VMEM((BLOCKS, FULL, n_tok), BF16),
@@ -529,6 +597,8 @@
             dma,
             dma,
             dma,
+            dma((4, 4)),
+            dma((4, 4)),
             dma((2, 2, 4)),
             dma((2, 2, 4)),
             dma((2, 2, 4)),

time: 150 us -> 141 us (0.940)
  the two profiles are of different devices: /device:TPU:48 before, /device:TPU:1 now
where the time goes in v5:
time: 141 us; the launch traced here: 140 us
  Pallas kernels  135 us (96%)
  local copies, waits for them, and re-layouts  4.38 us (3%)
    pallas_call x1, Pallas kernels, body(): pl.pallas_call(kernel, out_shape=(jax.ShapeDtypeStruct((n_tok, width), BF...  135 us
    unnamed x10, local copies, waits for them, and re-layouts  4.38 us

profile of v5, /device:TPU:1, one launch (start us, length us, event | category | flops | bytes accessed | tf_op | source)
XLA Modules:
  0.0 140.4 jit_solution(5647734612223889336)
XLA Ops:
  0.6 135.3 %moe_backward.1 = (bf16[128,1024]{1,0:T(8,128)(2,1)}, f32[1,128,384]{2,1,0:T(8,128)}, f32[1,128,384]{2,1,0:T(8,128)}, f32[1,384,128]{2,1,0:T(8,128)}) custom-call(bf16[128,1024]{1,0:T(8,128)(2,1)} %tok.1, bf16[128,1024]{1,0:T(8,128)(2,1)} %dout.1, f32[8,128]{1,0:T(8,128)} %bitcast.2, s32[8,128]{1,0:T(8,128)} %bitcast.3, bf16[1,128,384]{2,1,0:T(8,128)(2,1)} %gate.1, ...), custom_call_target="tpu_custom_call" | custom-call | tf_op jit(solution)/shard_map/moe_backward/pallas_call | solution.py:558
  136.0 0.0 copy-start.2
  136.0 1.7 %copy.15 = bf16[128,1024]{1,0:T(8,128)(2,1)} copy(bf16[128,1024]{1,0:T(8,128)(2,1)} %get-tuple-element.8) | data formatting | bytes 524288
  137.7 0.0 copy-done.2
  137.7 0.0 copy-start.1
  137.7 0.7 copy.16
  138.4 0.3 copy-done.1
  138.7 0.0 copy-start
  138.7 0.7 copy.17
  139.4 0.3 copy-done
  139.7 0.7 copy.18
Async XLA Ops:
  136.0 1.7 %copy-start.2 = (f32[1,128,384]{2,1,0:T(8,128)S(1)}, f32[1,128,384]{2,1,0:T(8,128)}, u32[]{:S(2)}) copy-start(f32[1,128,384]{2,1,0:T(8,128)} %get-tuple-element.9) | copy-start | bytes 589828
  137.7 1.0 copy-start.1
  138.7 1.0 copy-start

commit v6 on v5

--- a/solution.py
+++ b/solution.py
@@ -351,11 +351,11 @@
     own_picks()
     gather_next(1, 3)
 
-    def unpack(src, dst):
-        for b in range(2):
-            dst[b, :rows_main, :] = src[:, :, b * width : (b + 1) * width].reshape(
-                rows_main, width
-            )
+    def unpack_full(src, dst, b):
+        lanes = pl.ds(pl.multiple_of(b * width, width), width)
+        dst[b, :rows_main, :] = src[:, :, lanes].reshape(rows_main, width)
+
+    def unpack_rest(src, dst):
         rest = src[:, :, left:].reshape(rows_main, quarter)
         r = iota((4 * BLOCKS, rows_main), 0)
         base = ((r % (2 * BLOCKS)) // 2) * FULL + (r // (2 * BLOCKS)) * 2 + r % 2
@@ -368,7 +368,9 @@
                 ]
 
     whole(sx, rx, sem_xs, sem_xr, NEAR).wait_recv()
-    unpack(rx, xe)
+    unpack_rest(rx, xe)
+    for b in range(2):
+        unpack_full(rx, xe, b)
     for who in range(2):
         for d in range(2):
             gather_step(who, d, STEPS - 1, True).wait_recv()
@@ -444,10 +446,11 @@
         forward_rows(b)
 
     whole(sg, rg, sem_gs, sem_gr, NEAR).wait_recv()
-    unpack(rg, ge)
+    unpack_rest(rg, ge)
 
     for who in (1, 0):
         b = (b_own, b_oth)[who]
+        unpack_full(rg, ge, b)
         backward_rows(b)
         grads_of(b)
         if who == 0:
@@ -522,7 +525,7 @@
         one = jnp.where(q_pick == q, tail_pick.astype(F32), 0.0).astype(BF16)
         o_tok[:, q * quarter : (q + 1) * quarter] = (
             d_tok[:, q * quarter : (q + 1) * quarter] + dot_tn(one, tail)
-        ).astype(BF16)
+        )
 
     total = final(0)
     swap_grads.wait_recv()
@@ -555,10 +558,10 @@
     rows = BLOCKS * CAP
     vmem = pl.BlockSpec(memory_space=pltpu.VMEM)
     dma = pltpu.SemaphoreType.DMA
-    return pl.pallas_call(
+    d_tokens, d_gate, d_up, d_down = pl.pallas_call(
         kernel,
         out_shape=(
-            jax.ShapeDtypeStruct((n_tok, width), BF16),
+            jax.ShapeDtypeStruct((n_tok, width), F32),
             jax.ShapeDtypeStruct((1, shard, hid), F32),
             jax.ShapeDtypeStruct((1, shard, hid), F32),
             jax.ShapeDtypeStruct((1, hid, shard), F32),
@@ -611,6 +614,7 @@
         ),
         name="moe_backward",
     )(tokens, d_output, combine.T, routes.T, gate_weight, up_weight, down_weight)
+    return d_tokens.astype(BF16), d_gate, d_up, d_down
 
 
 def solution(mesh):

time: 141 us -> 141 us (level)
  other arithmetic: 0 us -> 1.82 us
  local copies, waits for them, and re-layouts: 4.38 us -> 2.67 us
    convert_element_type x0 -> x1, other arithmetic: none -> 1.82 us  [body(): return (d_tokens.astype(BF16), d_gate, d_up, d_down)]
    unnamed x10 -> x9, local copies, waits for them, and re-layouts: 4.38 us -> 2.67 us
where the time goes in v6:
time: 141 us; the launch traced here: 140 us
  Pallas kernels  135 us (96%)
  local copies, waits for them, and re-layouts  2.67 us (2%)
  other arithmetic  1.82 us (1%)
    pallas_call x1, Pallas kernels, body(): pl.pallas_call(kernel, out_shape=(jax.ShapeDtypeStruct((n_tok, width), F3...  135 us

profile of v6, /device:TPU:1, one launch (start us, length us, event | category | flops | bytes accessed | tf_op | source)
XLA Modules:
  0.0 140.5 jit_solution(15197483039887482136)
XLA Ops:
  0.6 135.4 %moe_backward.1 = (f32[128,1024]{1,0:T(8,128)}, f32[1,128,384]{2,1,0:T(8,128)}, f32[1,128,384]{2,1,0:T(8,128)}, f32[1,384,128]{2,1,0:T(8,128)}) custom-call(bf16[128,1024]{1,0:T(8,128)(2,1)} %tok.1, bf16[128,1024]{1,0:T(8,128)(2,1)} %dout.1, f32[8,128]{1,0:T(8,128)} %bitcast.2, s32[8,128]{1,0:T(8,128)} %bitcast.3, bf16[1,128,384]{2,1,0:T(8,128)(2,1)} %gate.1, ...), custom_call_target="tpu_custom_call" | custom-call | tf_op jit(solution)/shard_map/moe_backward/pallas_call | solution.py:561
  136.0 0.0 copy-start.2
  136.0 1.8 %convert_element_type.3 = bf16[128,1024]{1,0:T(8,128)(2,1)} convert(f32[128,1024]{1,0:T(8,128)} %get-tuple-element.8) | non-fusion elementwise | flops 131072 | bytes 786432 | tf_op jit(solution)/shard_map/convert_element_type | solution.py:617
  137.8 0.0 copy-done.2
  137.8 0.0 copy-start.1
  137.8 0.7 copy.14
  138.5 0.3 copy-done.1
  138.8 0.0 copy-start
  138.8 0.7 copy.15
  139.5 0.3 copy-done
  139.8 0.7 copy.16
Async XLA Ops:
  136.0 1.8 %copy-start.2 = (f32[1,128,384]{2,1,0:T(8,128)S(1)}, f32[1,128,384]{2,1,0:T(8,128)}, u32[]{:S(2)}) copy-start(f32[1,128,384]{2,1,0:T(8,128)} %get-tuple-element.17) | copy-start | bytes 589828
  137.8 1.0 copy-start.1
  138.8 1.0 copy-start
